TPU v7x, 32 devices: a whole 2x2x4 slice. The times are simulated.
32 devices in a mesh: lat: 2 (over x), lon: 4 (over z), mp: 4 (over y, core).
Axes of the slice: x: 2, y: 2, z: 4, core: 2. Of those that a mesh axis runs over, the one named last changes fastest.
Arguments:
- sharp_resolution_vectors: bfloat16 [2, 32, 64, 512], P(None, 'lat', 'lon'), may hold values from -6 to 6
- queries_keys_weights: bfloat16 [512, 2, 512], P(None, None, 'mp'), may hold values from -0.03125 to 0.03125
- values_weights: bfloat16 [512, 512], P(None, 'mp'), may hold values from -0.25 to 0.25
- attn_result_weights: bfloat16 [512, 512], P('mp'), may hold values from -0.75 to 0.75
- score_factors_by_lane: float32 [8], replicated, may hold values from 1 to 8
- tile_merging_weights: bfloat16 [2048, 1024], P('lon', 'mp'), may hold values from -0.125 to 0.125
- shrunk_dense_first: bfloat16 [1024, 4096], P('lon', 'mp'), may hold values from -0.1875 to 0.1875
- shrunk_dense_second: bfloat16 [4096, 1024], P('mp', 'lon'), may hold values from -0.09375 to 0.09375
- tile_unfolding_weights: bfloat16 [1024, 2048], P('lon', 'mp'), may hold values from -0.1875 to 0.1875
- result_gradient: bfloat16 [2, 32, 64, 512], P(None, 'lat', ('lon', 'mp')), may hold values from -6 to 6
Outputs:
- output: bfloat16 [2, 32, 64, 512], P(None, 'lat', ('lon', 'mp'))
- fine_grad: bfloat16 [2, 32, 64, 512], P(None, 'lat', ('lon', 'mp'))
All inputs are finite; a program needn't handle non-finite values.
Results may differ from a plain program's by a relative error of at most 0.02.
Values may be sent and summed in bfloat16 or wider, within the bound.
A program may use at most 128 MiB of HBM per device.

v0:
```python
import jax
import jax.numpy as jnp
from jax import lax
from jax.sharding import PartitionSpec as P

TILE_SIDE_CELLS = 8


epsilon = 1e-05


def shifted(value, axis, by):
    devices = lax.axis_size(axis)
    return lax.ppermute(value, axis, [(i, (i + by) % devices) for i in range(devices)])


def layer_norm(inputs):
    values = inputs.astype(jnp.float32)
    center = values - jnp.mean(values, -1, keepdims=True)
    spread = jnp.mean(center * center, -1, keepdims=True)
    return center * lax.rsqrt(spread + epsilon)


def norm_round(inputs):
    return layer_norm(inputs).astype(jnp.bfloat16)


def activate(inputs):
    return jax.nn.gelu(inputs.astype(jnp.float32)).astype(jnp.bfloat16)


def unit_rows(tensor):
    values = tensor.astype(jnp.float32)
    length = jnp.sqrt(jnp.sum(values * values, -1, keepdims=True))
    return (values / jnp.maximum(length, 1.0)).astype(jnp.bfloat16)


def window_attention(query_rows, key_rows, value_rows, scales, allowed):
    query_unit = lax.optimization_barrier(unit_rows(query_rows)).astype(jnp.float32)
    key_unit = lax.optimization_barrier(unit_rows(key_rows)).astype(jnp.float32)
    scores = scales[None, :, None, None] * jnp.einsum(
        "bthe,bshe->bhts", query_unit, key_unit, precision=lax.Precision.HIGHEST
    )
    weights_raw = jnp.where(allowed[:, None], jnp.exp(scores), 0.0)
    weights = lax.optimization_barrier(
        (weights_raw / jnp.sum(weights_raw, -1, keepdims=True)).astype(jnp.bfloat16)
    )
    weighted_sum_vectors = jnp.einsum(
        "bhts,bshe->bthe",
        weights.astype(jnp.float32),
        value_rows.astype(jnp.float32),
        precision=lax.Precision.HIGHEST,
    )
    return weighted_sum_vectors.astype(jnp.bfloat16)


def to_windows(tensor):
    levels, row_count, column_count, depth = tensor.shape
    tensor = tensor.reshape(
        levels,
        row_count // TILE_SIDE_CELLS,
        TILE_SIDE_CELLS,
        column_count // TILE_SIDE_CELLS,
        TILE_SIDE_CELLS,
        depth,
    ).transpose(1, 3, 0, 2, 4, 5)
    return tensor.reshape(
        row_count // TILE_SIDE_CELLS,
        column_count // TILE_SIDE_CELLS,
        levels * TILE_SIDE_CELLS * TILE_SIDE_CELLS,
        depth,
    )


def from_windows(tensor, levels):
    row_blocks, column_blocks, window_size, depth = tensor.shape
    tensor = tensor.reshape(
        row_blocks, column_blocks, levels, TILE_SIDE_CELLS, TILE_SIDE_CELLS, depth
    ).transpose(2, 0, 3, 1, 4, 5)
    return tensor.reshape(
        levels, row_blocks * TILE_SIDE_CELLS, column_blocks * TILE_SIDE_CELLS, depth
    )


def tile_normalized_averager(stacked, scales, shifted_zone_marks):
    levels = stacked.shape[0]
    heads = scales.shape[0]
    width = stacked.shape[3] // 3
    windows = to_windows(stacked)
    row_blocks, column_blocks, window_size = windows.shape[:3]
    window_count = row_blocks * column_blocks

    def select_part(part_index):
        return windows[..., part_index * width : (part_index + 1) * width].reshape(
            window_count, window_size, heads, width // heads
        )

    token_label = jnp.broadcast_to(
        shifted_zone_marks.reshape(row_blocks, 1, TILE_SIDE_CELLS, 1),
        (row_blocks, levels, TILE_SIDE_CELLS, TILE_SIDE_CELLS),
    ).reshape(row_blocks, window_size)
    allowed = token_label[:, :, None] == token_label[:, None, :]
    allowed = jnp.broadcast_to(
        allowed[:, None], (row_blocks, column_blocks, window_size, window_size)
    ).reshape(window_count, window_size, window_size)
    weighted_sum_vectors = window_attention(
        select_part(0), select_part(1), select_part(2), scales, allowed
    )
    return from_windows(
        weighted_sum_vectors.reshape(row_blocks, column_blocks, window_size, width), levels
    )


def combined_normalizer(latent_finer_state):
    levels, row_count, column_count, width = latent_finer_state.shape
    grouped = latent_finer_state.reshape(
        levels, row_count // 2, 2, column_count // 2, 2, width
    ).transpose(0, 1, 3, 2, 4, 5)
    grouped = grouped.reshape(levels, row_count // 2, column_count // 2, 4 * width)
    return layer_norm(grouped).astype(jnp.bfloat16)


def roll_ahead(tensor):
    half_win = TILE_SIDE_CELLS // 2
    incoming = shifted(tensor[:, :half_win], "lat", -1)
    tensor = jnp.concatenate([tensor[:, half_win:], incoming], 1)
    incoming = shifted(tensor[:, :, :half_win], "lon", -1)
    return jnp.concatenate([tensor[:, :, half_win:], incoming], 2)


def roll_back(tensor):
    half_win = TILE_SIDE_CELLS // 2
    incoming = shifted(tensor[:, :, -half_win:], "lon", 1)
    tensor = jnp.concatenate([incoming, tensor[:, :, :-half_win]], 2)
    incoming = shifted(tensor[:, -half_win:], "lat", 1)
    return jnp.concatenate([incoming, tensor[:, :-half_win]], 1)


def per_device(
    sharp_resolution_vectors,
    queries_keys_weights,
    values_weights,
    attn_result_weights,
    score_factors_by_lane,
    tile_merging_weights,
    shrunk_dense_first,
    shrunk_dense_second,
    tile_unfolding_weights,
    result_gradient,
):
    levels, row_count, column_count, width = sharp_resolution_vectors.shape
    longitude_slice_size = lax.axis_size("mp")
    processor_position = lax.axis_index("mp")
    column_share = column_count // longitude_slice_size
    row_total = row_count * lax.axis_size("lat")
    position = lax.axis_index("lat") * row_count + jnp.arange(row_count, dtype=jnp.int32)
    shifted_zone_marks = (position >= row_total - TILE_SIDE_CELLS).astype(jnp.int32) + (
        position >= row_total - TILE_SIDE_CELLS // 2
    ).astype(jnp.int32)
    own_fine = lax.dynamic_slice_in_dim(
        sharp_resolution_vectors, processor_position * column_share, column_share, 2
    )
    local_width = values_weights.shape[1]
    features_on_processor = score_factors_by_lane.shape[0] // longitude_slice_size
    scale_share_local = lax.dynamic_slice_in_dim(
        score_factors_by_lane, processor_position * features_on_processor, features_on_processor, 0
    )
    joined = jnp.concatenate(
        [queries_keys_weights.reshape(width, 2 * local_width), values_weights], 1
    )
    source = roll_ahead(sharp_resolution_vectors)
    normed, norm_pull = jax.vjp(norm_round, source)
    stacked = jnp.dot(normed, joined, preferred_element_type=jnp.float32).astype(jnp.bfloat16)
    weighted_sum_vectors, attend_pull = jax.vjp(
        lambda packed: tile_normalized_averager(packed, scale_share_local, shifted_zone_marks),
        stacked,
    )
    mixed_back = roll_back(weighted_sum_vectors)
    partial_out = jnp.dot(mixed_back, attn_result_weights, preferred_element_type=jnp.float32)
    summed = lax.psum_scatter(
        partial_out.astype(jnp.bfloat16), "mp", scatter_dimension=2, tiled=True
    ).astype(jnp.float32)
    latent_finer_state = (own_fine.astype(jnp.float32) + summed).astype(jnp.bfloat16)
    merged_in, merge_pull = jax.vjp(combined_normalizer, latent_finer_state)
    gathered_in = lax.all_gather(merged_in, "mp", axis=2, tiled=True)
    coarse_in = gathered_in.reshape(-1, 4 * width)
    coarse_count = coarse_in.shape[0]
    stripe_span = tile_merging_weights.shape[1]
    merge_full, inner_full, outer_full, expand_full = (
        lax.all_gather(tile_merging_weights, "lon", axis=0, tiled=True),
        lax.all_gather(shrunk_dense_first, "lon", axis=0, tiled=True),
        lax.all_gather(shrunk_dense_second, "lon", axis=1, tiled=True),
        lax.all_gather(tile_unfolding_weights, "lon", axis=0, tiled=True),
    )
    merged_columns = jnp.dot(coarse_in, merge_full, preferred_element_type=jnp.float32)
    reduced_level = lax.all_gather(merged_columns.astype(jnp.bfloat16), "mp", axis=1, tiled=True)
    coarse_norm, coarse_pull = jax.vjp(norm_round, reduced_level)
    inner = jnp.dot(coarse_norm, inner_full, preferred_element_type=jnp.float32)
    activated, activate_pull = jax.vjp(activate, inner.astype(jnp.bfloat16))
    outer = jnp.dot(activated, outer_full, preferred_element_type=jnp.float32)
    hidden_sum = lax.psum(outer.astype(jnp.bfloat16), "mp").astype(jnp.float32)
    coarse_out = (reduced_level.astype(jnp.float32) + hidden_sum).astype(jnp.bfloat16)
    expanded = jnp.dot(coarse_out, expand_full, preferred_element_type=jnp.float32)
    expanded = expanded.astype(jnp.bfloat16).reshape(
        levels, row_count // 2, column_count // 2, 1, width
    )
    moved = lax.all_to_all(expanded, "mp", split_axis=2, concat_axis=3, tiled=True)
    fine_added = moved.reshape(levels, row_count // 2, column_share // 2, 2, 2, width).transpose(
        0, 1, 3, 2, 4, 5
    )
    fine_added = fine_added.reshape(levels, row_count, column_share, width)
    output = (latent_finer_state.astype(jnp.float32) + fine_added.astype(jnp.float32)).astype(
        jnp.bfloat16
    )
    delta_sub = result_gradient.reshape(
        levels, row_count // 2, 2, column_share // 2, 2, width
    ).transpose(0, 1, 3, 2, 4, 5)
    delta_sub = delta_sub.reshape(
        levels, row_count // 2, column_share // 2, longitude_slice_size, width
    )
    delta_expand = lax.all_to_all(delta_sub, "mp", split_axis=3, concat_axis=2, tiled=True).reshape(
        coarse_count, width
    )
    delta_out_part = jnp.dot(delta_expand, expand_full.T, preferred_element_type=jnp.float32)
    delta_coarse_out = lax.psum(delta_out_part.astype(jnp.bfloat16), "mp")
    delta_active = jnp.dot(delta_coarse_out, outer_full.T, preferred_element_type=jnp.float32)
    delta_inner = activate_pull(delta_active.astype(jnp.bfloat16))[0]
    delta_norm_part = jnp.dot(delta_inner, inner_full.T, preferred_element_type=jnp.float32)
    delta_norm = lax.psum(delta_norm_part.astype(jnp.bfloat16), "mp")
    delta_coarse = (
        delta_coarse_out.astype(jnp.float32) + coarse_pull(delta_norm)[0].astype(jnp.float32)
    ).astype(jnp.bfloat16)
    delta_columns = lax.dynamic_slice_in_dim(
        delta_coarse, processor_position * stripe_span, stripe_span, 1
    )
    delta_merge_part = jnp.dot(delta_columns, merge_full.T, preferred_element_type=jnp.float32)
    delta_merge_part = delta_merge_part.reshape(
        levels, row_count // 2, column_count // 2, 4 * width
    )
    delta_merged = lax.psum_scatter(
        delta_merge_part.astype(jnp.bfloat16), "mp", scatter_dimension=2, tiled=True
    )
    delta_hidden_merge = merge_pull(delta_merged)[0]
    delta_hidden = (
        result_gradient.astype(jnp.float32) + delta_hidden_merge.astype(jnp.float32)
    ).astype(jnp.bfloat16)
    delta_mixed_back = jnp.dot(
        lax.all_gather(delta_hidden, "mp", axis=2, tiled=True),
        attn_result_weights.T,
        preferred_element_type=jnp.float32,
    ).astype(jnp.bfloat16)
    delta_mixed = roll_ahead(delta_mixed_back)
    delta_stacked = attend_pull(delta_mixed)[0]
    delta_normed_part = jnp.dot(delta_stacked, joined.T, preferred_element_type=jnp.float32)
    delta_normed = lax.psum(delta_normed_part.astype(jnp.bfloat16), "mp")
    delta_source = norm_pull(delta_normed)[0]
    delta_source = roll_back(delta_source)
    own_delta = lax.dynamic_slice_in_dim(
        delta_source, processor_position * column_share, column_share, 2
    )
    fine_grad = (delta_hidden.astype(jnp.float32) + own_delta.astype(jnp.float32)).astype(
        jnp.bfloat16
    )
    return (output, fine_grad)


def solution(mesh):
    in_specs = (
        P(None, "lat", "lon", None),
        P(None, None, "mp"),
        P(None, "mp"),
        P("mp", None),
        P(),
        P("lon", "mp"),
        P("lon", "mp"),
        P("mp", "lon"),
        P("lon", "mp"),
        P(None, "lat", ("lon", "mp"), None),
    )
    out_specs = (P(None, "lat", ("lon", "mp"), None), P(None, "lat", ("lon", "mp"), None))
    return jax.shard_map(
        per_device, mesh=mesh, in_specs=in_specs, out_specs=out_specs, check_vma=False
    )
```

profile of v0, /device:TPU:0, one launch (start us, length us, event | category | flops | bytes accessed | tf_op | source)
XLA Modules:
  0.0 326.0 jit_solution(6486134108233316506)
XLA Ops:
  9.1 3.0 collective-permute-start
  13.4 2.2 collective-permute-done
  15.6 3.9 %collective-permute-start.1 = (bf16[2,16,4,512]{3,2,1,0:T(4,128)(2,1)S(1)}, bf16[2,16,4,512]{3,2,1,0:T(4,128)(2,1)S(1)}, u32[]{:S(2)}, u32[]{:S(2)}) collective-permute-start(bf16[2,16,4,512]{3,2,1,0:T(4,128)(2,1)S(1)} %pad_maximum_fusion.3), channel_id=1, source_target_pairs={{0,12},{4,0},{8,4},{12,8},{1,13},{5,1},{9,5},{13,9},{2,14},{6,2},{... | collective-permute-start | bytes 393224 | tf_op jit(solution)/shard_map/ppermute | solution.py:14
  19.9 3.7 %collective-permute-done.1 = bf16[2,16,4,512]{3,2,1,0:T(4,128)(2,1)S(1)} collective-permute-done((bf16[2,16,4,512]{3,2,1,0:T(4,128)(2,1)S(1)}, bf16[2,16,4,512]{3,2,1,0:T(4,128)(2,1)S(1)}, u32[]{:S(2)}, u32[]{:S(2)}) %collective-permute-start.1) | collective-permute-done | bytes 131104 | tf_op jit(solution)/shard_map/ppermute | solution.py:14
  28.1 7.0 %collective-permute-done.2 = bf16[2,16,4,128]{3,2,1,0:T(4,128)(2,1)S(1)} collective-permute-done((bf16[2,16,4,128]{3,2,1,0:T(4,128)(2,1)S(1)}, bf16[2,16,4,128]{3,2,1,0:T(4,128)(2,1)S(1)}, u32[]{:S(2)}, u32[]{:S(2)}) %collective-permute-start.2) | collective-permute-done | bytes 32800 | tf_op jit(solution)/shard_map/ppermute | solution.py:14
  36.2 2.9 collective-permute-done.3
  42.3 7.0 %all_to_all.27 = bf16[2,8,2,4,512]{4,1,2,0,3:T(8,128)(2,1)S(1)} all-to-all(bf16[2,8,2,4,512]{4,1,2,0,3:T(8,128)(2,1)S(1)} %bitcast.158), channel_id=1, replica_groups=mesh['lat'=2,'lon'=4,'mp'=4] {'mp'}, dimensions={3} | all-to-all | bytes 262144 | tf_op jit(solution)/shard_map/all_to_all | solution.py:221
  49.5 2.4 convolution_convert_fusion.7
  53.6 8.7 %reduce-scatter.5.cloned.1.call-done = bf16[2,16,4,512]{3,1,0,2:T(8,128)(2,1)} async-done(((bf16[2,16,16,512]{3,1,0,2:T(8,128)(2,1)}), bf16[2,16,4,512]{3,1,0,2:T(8,128)(2,1)}) %reduce-scatter.5.cloned.1.call-update) | async-done | bytes 131088 | tf_op jit(solution)/shard_map/reduce_scatter | solution.py:180
  64.5 6.6 %all_gather.21 = bf16[2,8,8,2048]{3,1,2,0:T(8,128)(2,1)S(1)} all-gather(bf16[2,8,2,2048]{3,1,2,0:T(8,128)(2,1)S(1)} %multiply_convert_fusion.2), channel_id=1, replica_groups=mesh['lat'=2,'lon'=4,'mp'=4] {'mp'}, dimensions={2}, use_global_device_ids=true | all-gather | bytes 655360 | tf_op jit(solution)/shard_map/all_gather | solution.py:185
  73.0 5.8 %all_gather.23 = bf16[128,1024]{1,0:T(8,128)(2,1)S(1)} all-gather(bf16[128,256]{1,0:T(8,128)(2,1)S(1)} %convolution_convert_fusion.16), channel_id=1, replica_groups=mesh['lat'=2,'lon'=4,'mp'=4] {'mp'}, dimensions={1}, use_global_device_ids=true | all-gather | bytes 327680 | tf_op jit(solution)/shard_map/all_gather | solution.py:196
  79.2 38.9 %all-gather.7.cloned.1.call-done = bf16[1024,1024]{1,0:T(8,128)(2,1)} async-done(((bf16[256,1024]{1,0:T(8,128)(2,1)}), bf16[1024,1024]{1,0:T(8,128)(2,1)}) %all-gather.7.cloned.1.call-update) | async-done | bytes 2097168 | tf_op jit(solution)/shard_map/all_gather | solution.py:191
  118.1 2.1 fusion.5
  120.2 44.4 %all-gather.9.cloned.1.call-done = bf16[1024,1024]{1,0:T(8,128)(2,1)} async-done(((bf16[1024,256]{1,0:T(8,128)(2,1)}), bf16[1024,1024]{1,0:T(8,128)(2,1)}) %all-gather.9.cloned.1.call-update) | async-done | bytes 2097168 | tf_op jit(solution)/shard_map/all_gather | solution.py:192
  164.6 4.7 %convolution_convert_fusion.5 = bf16[128,1024]{1,0:T(8,128)(2,1)} fusion(bf16[1024,1024]{1,0:T(8,128)(2,1)} %all-gather.7.cloned.1.call-done, f32[128,1024]{1,0:T(8,128)S(1)} %fusion.5, bf16[128,1024]{1,0:T(8,128)(2,1)} %all-reduce.10.cloned.1.call-done, bf16[1024,1024]{1,0:T(8,128)(2,1)} %all-gather.9.cloned.1.call-done), kind=kOutput, calls=%fused_computation.15 | convolution fusion | flops 539885568 | bytes 5242880 | tf_op jit(solution)/shard_map/dot_general | solution.py:228
  169.4 30.2 %all-reduce.12.cloned.1.call-done = bf16[128,1024]{1,0:T(8,128)(2,1)} async-done(((bf16[128,1024]{1,0:T(8,128)(2,1)}), bf16[128,1024]{1,0:T(8,128)(2,1)}) %all-reduce.12.cloned.1.call-update) | async-done | bytes 262160 | tf_op jit(solution)/shard_map/psum | solution.py:229
  208.3 30.3 %all-reduce.14.cloned.1.call-done = bf16[2,8,8,2048]{3,1,2,0:T(8,128)(2,1)} async-done(((bf16[2,8,8,2048]{3,1,2,0:T(8,128)(2,1)}), bf16[2,8,8,2048]{3,1,2,0:T(8,128)(2,1)}) %all-reduce.14.cloned.1.call-update) | async-done | bytes 524304
  242.4 6.8 %all_gather.27 = bf16[2,16,16,512]{3,1,0,2:T(8,128)(2,1)S(1)} all-gather(bf16[2,16,4,512]{3,1,0,2:T(8,128)(2,1)S(1)} %copy.124), channel_id=1, replica_groups=mesh['lat'=2,'lon'=4,'mp'=4] {'mp'}, dimensions={2}, use_global_device_ids=true | all-gather | bytes 655360 | tf_op jit(solution)/shard_map/all_gather | solution.py:248
  253.6 3.4 %collective-permute-start.5 = (bf16[2,16,4,128]{3,2,1,0:T(4,128)(2,1)S(1)}, bf16[2,16,4,128]{3,2,1,0:T(4,128)(2,1)S(1)}, u32[]{:S(2)}, u32[]{:S(2)}) collective-permute-start(bf16[2,16,4,128]{3,2,1,0:T(4,128)(2,1)S(1)} %pad_maximum_fusion.5), channel_id=1, source_target_pairs={{0,12},{4,0},{8,4},{12,8},{1,13},{5,1},{9,5},{13,9},{2,14},{6,2},{... | collective-permute-start | bytes 98312 | tf_op jit(solution)/shard_map/ppermute | solution.py:14
  263.3 36.4 %all-reduce.16.cloned.1.call-done = (bf16[128,1024]{1,0:T(8,128)(2,1)}, bf16[2,16,16,512]{3,2,1,0:T(8,128)(2,1)}) async-done(((bf16[128,1024]{1,0:T(8,128)(2,1)}, bf16[2,16,16,512]{3,2,1,0:T(8,128)(2,1)}), (bf16[128,1024]{1,0:T(8,128)(2,1)}, bf16[2,16,16,512]{3,2,1,0:T(8,128)(2,1)})) %all-reduce.16.cloned.1.call-update) | async-done | bytes 786448 | tf_op jit(solution)/shard_map/psum | solution.py:201
  299.6 1.6 fusion.11
  301.2 1.6 fusion.16
  305.4 7.0 %all_to_all.28 = bf16[2,8,8,1,512]{4,1,0,3,2:T(8,128)(2,1)S(1)} all-to-all(bf16[2,8,8,1,512]{4,1,0,3,2:T(8,128)(2,1)S(1)} %copy.114), channel_id=1, replica_groups=mesh['lat'=2,'lon'=4,'mp'=4] {'mp'}, dimensions={2} | all-to-all | bytes 262144 | tf_op jit(solution)/shard_map/all_to_all | solution.py:207
  315.2 2.5 collective-permute-done.7
  (207 shorter events, 45.9 us)
Async XLA Ops:
  8.0 31.1 %copy-start = (bf16[128,512]{1,0:T(8,128)(2,1)S(1)}, bf16[128,512]{1,0:T(8,128)(2,1)}, u32[]{:S(2)}) copy-start(bf16[128,512]{1,0:T(8,128)(2,1)} %param.13) | copy-start | bytes 393220
  8.0 41.4 %all-gather.11.cloned.1.call-start = ((), (), s32[]{:S(2)}) async-start(), calls=%async_computation.7 | async-start | bytes 1310720 | tf_op jit(solution)/shard_map/all_gather | solution.py:193
  9.1 6.5 %collective-permute-start = (bf16[2,4,16,512]{3,2,1,0:T(8,128)(2,1)S(1)}, bf16[2,4,16,512]{3,2,1,0:T(8,128)(2,1)S(1)}, u32[]{:S(2)}, u32[]{:S(2)}) collective-permute-start(bf16[2,4,16,512]{3,2,1,0:T(8,128)(2,1)S(1)} %slice.58), channel_id=1, source_target_pairs={{0,16},{16,0},{1,17},{17,1},{2,18},{18,2},{3,19},{19,3},{4,20},{20... | collective-permute-start | bytes 393224 | tf_op jit(solution)/shard_map/ppermute | solution.py:14
  12.1 50.2 %reduce-scatter.5.cloned.1.call-start = ((), (), s32[]{:S(2)}) async-start(), calls=%async_computation.3 | async-start | bytes 655360 | tf_op jit(solution)/shard_map/reduce_scatter | solution.py:180
  15.6 8.0 %collective-permute-start.1 = (bf16[2,16,4,512]{3,2,1,0:T(4,128)(2,1)S(1)}, bf16[2,16,4,512]{3,2,1,0:T(4,128)(2,1)S(1)}, u32[]{:S(2)}, u32[]{:S(2)}) collective-permute-start(bf16[2,16,4,512]{3,2,1,0:T(4,128)(2,1)S(1)} %pad_maximum_fusion.3), channel_id=1, source_target_pairs={{0,12},{4,0},{8,4},{12,8},{1,13},{5,1},{9,5},{13,9},{2,14},{6,2},{... | collective-permute-start | bytes 393224 | tf_op jit(solution)/shard_map/ppermute | solution.py:14
  28.0 7.1 %collective-permute-start.2 = (bf16[2,16,4,128]{3,2,1,0:T(4,128)(2,1)S(1)}, bf16[2,16,4,128]{3,2,1,0:T(4,128)(2,1)S(1)}, u32[]{:S(2)}, u32[]{:S(2)}) collective-permute-start(bf16[2,16,4,128]{3,2,1,0:T(4,128)(2,1)S(1)} %slice.81), channel_id=1, source_target_pairs={{0,4},{4,8},{8,12},{12,0},{1,5},{5,9},{9,13},{13,1},{2,6},{6,10},{... | collective-permute-start | bytes 98312 | tf_op jit(solution)/shard_map/ppermute | solution.py:14
  35.1 4.0 %collective-permute-start.3 = (bf16[2,4,16,128]{3,2,1,0:T(8,128)(2,1)S(1)}, bf16[2,4,16,128]{3,2,1,0:T(8,128)(2,1)S(1)}, u32[]{:S(2)}, u32[]{:S(2)}) collective-permute-start(bf16[2,4,16,128]{3,2,1,0:T(8,128)(2,1)S(1)} %pad_maximum_fusion.6), channel_id=1, source_target_pairs={{0,16},{16,0},{1,17},{17,1},{2,18},{18,2},{3,19},{19,3},{4,20},{20... | collective-permute-start | bytes 98312 | tf_op jit(solution)/shard_map/ppermute | solution.py:14
  40.5 30.9 %all-gather.5.cloned.1.call-start = ((), (), s32[]{:S(2)}) async-start(), calls=%async_computation.4 | async-start | bytes 1310720 | tf_op jit(solution)/shard_map/all_gather | solution.py:190
  41.3 76.8 %all-gather.7.cloned.1.call-start = ((), (), s32[]{:S(2)}) async-start(), calls=%async_computation.5 | async-start | bytes 2621440 | tf_op jit(solution)/shard_map/all_gather | solution.py:191
  42.0 78.2 %all-reduce.10.cloned.1.call-start = ((), (), s32[]{:S(2)}) async-start(), calls=%async_computation.8 | async-start | bytes 524288 | tf_op jit(solution)/shard_map/psum | solution.py:225
  51.9 112.7 %all-gather.9.cloned.1.call-start = ((), (), s32[]{:S(2)}) async-start(), calls=%async_computation.6 | async-start | bytes 2621440 | tf_op jit(solution)/shard_map/all_gather | solution.py:192
  52.5 147.1 %all-reduce.12.cloned.1.call-start = ((), (), s32[]{:S(2)}) async-start(), calls=%async_computation.9 | async-start | bytes 524288 | tf_op jit(solution)/shard_map/psum | solution.py:229
  78.9 85.7 %copy-start.23 = (f32[128]{0:T(128)}, f32[128]{0:T(128)S(1)}, u32[]{:S(2)}) copy-start(f32[128]{0:T(128)S(1)} %broadcast_multiply_fusion.2) | copy-start | bytes 1540
  79.2 85.5 %copy-start.25 = (f32[128]{0:T(128)}, f32[128]{0:T(128)S(1)}, u32[]{:S(2)}) copy-start(f32[128]{0:T(128)S(1)} %fusion.30) | copy-start | bytes 1540
  79.2 85.4 %copy-start.24 = (f32[128]{0:T(128)}, f32[128]{0:T(128)S(1)}, u32[]{:S(2)}) copy-start(f32[128]{0:T(128)S(1)} %fusion.84) | copy-start | bytes 1540
  120.2 44.4 %copy-start.9 = (f32[128,1024]{1,0:T(8,128)}, f32[128,1024]{1,0:T(8,128)S(1)}, u32[]{:S(2)}) copy-start(f32[128,1024]{1,0:T(8,128)S(1)} %fusion.5) | copy-start | bytes 1572868
  169.3 33.4 %copy-start.2 = (bf16[2048,256]{1,0:T(8,128)(2,1)S(1)}, bf16[2048,256]{1,0:T(8,128)(2,1)}, u32[]{:S(2)}) copy-start(bf16[2048,256]{1,0:T(8,128)(2,1)} %all-gather.5.cloned.1.call-done) | copy-start | bytes 3145732
  169.3 69.2 %all-reduce.14.cloned.1.call-start = ((), (), s32[]{:S(2)}) async-start(), calls=%async_computation.10 | async-start | bytes 1048576
  204.0 38.2 %copy-start.8 = (bf16[2,16,4,512]{3,2,1,0:T(4,128)(2,1)S(1)}, bf16[2,16,4,512]{3,2,1,0:T(4,128)(2,1)}, u32[]{:S(2)}) copy-start(bf16[2,16,4,512]{3,2,1,0:T(4,128)(2,1)} %param.19) | copy-start | bytes 393220
  205.1 94.5 %all-reduce.16.cloned.1.call-start = ((), (), s32[]{:S(2)}) async-start(), calls=%async_computation.11 | async-start | bytes 1572864 | tf_op jit(solution)/shard_map/psum | solution.py:201
  249.6 4.0 %collective-permute-start.4 = (bf16[2,4,16,128]{3,2,1,0:T(8,128)(2,1)S(1)}, bf16[2,4,16,128]{3,2,1,0:T(8,128)(2,1)S(1)}, u32[]{:S(2)}, u32[]{:S(2)}) collective-permute-start(bf16[2,4,16,128]{3,2,1,0:T(8,128)(2,1)S(1)} %slice.84), channel_id=1, source_target_pairs={{0,16},{16,0},{1,17},{17,1},{2,18},{18,2},{3,19},{19,3},{4,20},{20... | collective-permute-start | bytes 98312 | tf_op jit(solution)/shard_map/ppermute | solution.py:14
  253.6 5.0 %collective-permute-start.5 = (bf16[2,16,4,128]{3,2,1,0:T(4,128)(2,1)S(1)}, bf16[2,16,4,128]{3,2,1,0:T(4,128)(2,1)S(1)}, u32[]{:S(2)}, u32[]{:S(2)}) collective-permute-start(bf16[2,16,4,128]{3,2,1,0:T(4,128)(2,1)S(1)} %pad_maximum_fusion.5), channel_id=1, source_target_pairs={{0,12},{4,0},{8,4},{12,8},{1,13},{5,1},{9,5},{13,9},{2,14},{6,2},{... | collective-permute-start | bytes 98312 | tf_op jit(solution)/shard_map/ppermute | solution.py:14
  303.5 9.2 %collective-permute-start.6 = (bf16[2,16,4,512]{3,2,1,0:T(4,128)(2,1)S(1)}, bf16[2,16,4,512]{3,2,1,0:T(4,128)(2,1)S(1)}, u32[]{:S(2)}, u32[]{:S(2)}) collective-permute-start(bf16[2,16,4,512]{3,2,1,0:T(4,128)(2,1)S(1)} %slice.87), channel_id=1, source_target_pairs={{0,4},{4,8},{8,12},{12,0},{1,5},{5,9},{9,13},{13,1},{2,6},{6,10},{... | collective-permute-start | bytes 393224 | tf_op jit(solution)/shard_map/ppermute | solution.py:14
  312.7 5.0 %collective-permute-start.7 = (bf16[2,4,16,512]{3,2,1,0:T(8,128)(2,1)S(1)}, bf16[2,4,16,512]{3,2,1,0:T(8,128)(2,1)S(1)}, u32[]{:S(2)}, u32[]{:S(2)}) collective-permute-start(bf16[2,4,16,512]{3,2,1,0:T(8,128)(2,1)S(1)} %pad_maximum_fusion.1), channel_id=1, source_target_pairs={{0,16},{16,0},{1,17},{17,1},{2,18},{18,2},{3,19},{19,3},{4,20},{20... | collective-permute-start | bytes 393224 | tf_op jit(solution)/shard_map/ppermute | solution.py:14
  (25 other events, 161.1 us)
Sparse Core Ops, SparseCore 0:
  12.2 29.5 all-gather.10
  43.4 27.9 all-gather.4
  73.0 45.0 all-gather.6
  119.5 45.0 all-gather.8
Sparse Core Ops, SparseCore 1:
  40.6 21.6 reduce-scatter.4
  64.5 32.0 all-reduce.9
  169.4 30.1 all-reduce.11
  205.2 33.3 all-reduce.13
  263.4 36.2 all-reduce.15
where the time goes:
time: 327 us; the launch traced here: 326 us
  waiting for transfers between devices  212 us (65%)
  blocking collectives  33.2 us (10%)
  matrix products  18.3 us (6%)
  other arithmetic  17.2 us (5%)
  between operations  17 us (5%)
  starting transfers between devices  16.4 us (5%)
  local copies, waits for them, and re-layouts  11.8 us (4%)
    all_gather x1, waiting for transfers between devices, per_device(): lax.all_gather(shrunk_dense_second, 'lon', axis=1, tiled=True)  44.4 us
    all_gather x1, waiting for transfers between devices, per_device(): lax.all_gather(shrunk_dense_first, 'lon', axis=0, tiled=True)  38.9 us
    psum x1, waiting for transfers between devices, per_device(): hidden_sum = lax.psum(outer.astype(jnp.bfloat16), 'mp').astype(jnp.float32)  36.4 us
    unnamed x10, waiting for transfers between devices  32.3 us
    psum x1, waiting for transfers between devices, per_device(): delta_norm = lax.psum(delta_norm_part.astype(jnp.bfloat16), 'mp')  30.2 us
    ppermute x8, waiting for transfers between devices, shifted(): lax.ppermute(value, axis, [(i, (i + by) % devices) for i in range(devices)])  21.1 us
    ppermute x8, starting transfers between devices, shifted(): lax.ppermute(value, axis, [(i, (i + by) % devices) for i in range(devices)])  16 us
    reduce_scatter x1, waiting for transfers between devices, per_device(): lax.psum_scatter(partial_out.astype(jnp.bfloat16), 'mp', scatter_dimensio...  8.7 us
  transfers between devices with their start and end apart: 17, of which 14 were waited for; matrix products, arithmetic and copies ran while one was open for 7% of the time, Pallas kernels for 0%

commit v1 on v0

--- a/solution.py
+++ b/solution.py
@@ -134,6 +134,32 @@
     tensor = jnp.concatenate([incoming, tensor[:, :, :-half_win]], 2)
     incoming = shifted(tensor[:, -half_win:], "lat", 1)
     return jnp.concatenate([incoming, tensor[:, :-half_win]], 1)
+
+
+def gather_blocks(value, axis):
+    devices = lax.axis_size(axis)
+    pieces = [value] + [shifted(value, axis, by) for by in range(1, devices)]
+    return pieces
+
+
+def turn(value, blocks, by):
+    rows, features = value.shape
+    order = jnp.mod(by - jnp.arange(blocks), blocks)
+    parts = value.reshape(rows, blocks, features // blocks)
+    pieces = [lax.dynamic_index_in_dim(parts, order[k], 1, False) for k in range(blocks)]
+    return jnp.concatenate(pieces, 1)
+
+
+def sum_scatter(value, axis):
+    moved = lax.all_to_all(value, axis, split_axis=0, concat_axis=0, tiled=True)
+    return jnp.sum(moved.astype(jnp.float32), 0)
+
+
+def sum_all(value, axis):
+    devices = lax.axis_size(axis)
+    rows, features = value.shape
+    own = sum_scatter(value.reshape(devices, rows // devices, features), axis)
+    return lax.all_gather(own.astype(value.dtype), axis, axis=0, tiled=True)
 
 
 def per_device(
@@ -157,6 +183,15 @@
     shifted_zone_marks = (position >= row_total - TILE_SIDE_CELLS).astype(jnp.int32) + (
         position >= row_total - TILE_SIDE_CELLS // 2
     ).astype(jnp.int32)
+
+    def columns_first(value):
+        lev, rows, columns, feats = value.shape
+        return jnp.moveaxis(
+            value.reshape(lev, rows, longitude_slice_size, columns // longitude_slice_size, feats),
+            2,
+            0,
+        )
+
     own_fine = lax.dynamic_slice_in_dim(
         sharp_resolution_vectors, processor_position * column_share, column_share, 2
     )
@@ -177,28 +212,26 @@
     )
     mixed_back = roll_back(weighted_sum_vectors)
     partial_out = jnp.dot(mixed_back, attn_result_weights, preferred_element_type=jnp.float32)
-    summed = lax.psum_scatter(
-        partial_out.astype(jnp.bfloat16), "mp", scatter_dimension=2, tiled=True
-    ).astype(jnp.float32)
+    summed = sum_scatter(columns_first(partial_out.astype(jnp.bfloat16)), "mp")
     latent_finer_state = (own_fine.astype(jnp.float32) + summed).astype(jnp.bfloat16)
     merged_in, merge_pull = jax.vjp(combined_normalizer, latent_finer_state)
     gathered_in = lax.all_gather(merged_in, "mp", axis=2, tiled=True)
-    coarse_in = gathered_in.reshape(-1, 4 * width)
+    coarse_in = turn(gathered_in.reshape(-1, 4 * width), lax.axis_size("lon"), lax.axis_index("lon"))
     coarse_count = coarse_in.shape[0]
     stripe_span = tile_merging_weights.shape[1]
-    merge_full, inner_full, outer_full, expand_full = (
-        lax.all_gather(tile_merging_weights, "lon", axis=0, tiled=True),
-        lax.all_gather(shrunk_dense_first, "lon", axis=0, tiled=True),
-        lax.all_gather(shrunk_dense_second, "lon", axis=1, tiled=True),
-        lax.all_gather(tile_unfolding_weights, "lon", axis=0, tiled=True),
-    )
+    lon_count, lon_here = lax.axis_size("lon"), lax.axis_index("lon")
+    merge_full = jnp.concatenate(gather_blocks(tile_merging_weights, "lon"), 0)
+    inner_full = jnp.concatenate(gather_blocks(shrunk_dense_first, "lon"), 0)
+    outer_full = jnp.concatenate(gather_blocks(shrunk_dense_second, "lon"), 1)
+    expand_full = jnp.concatenate(gather_blocks(tile_unfolding_weights, "lon"), 0)
     merged_columns = jnp.dot(coarse_in, merge_full, preferred_element_type=jnp.float32)
     reduced_level = lax.all_gather(merged_columns.astype(jnp.bfloat16), "mp", axis=1, tiled=True)
+    reduced_level = turn(reduced_level, lon_count, lon_here)
     coarse_norm, coarse_pull = jax.vjp(norm_round, reduced_level)
     inner = jnp.dot(coarse_norm, inner_full, preferred_element_type=jnp.float32)
     activated, activate_pull = jax.vjp(activate, inner.astype(jnp.bfloat16))
     outer = jnp.dot(activated, outer_full, preferred_element_type=jnp.float32)
-    hidden_sum = lax.psum(outer.astype(jnp.bfloat16), "mp").astype(jnp.float32)
+    hidden_sum = sum_all(outer.astype(jnp.bfloat16), "mp").astype(jnp.float32)
     coarse_out = (reduced_level.astype(jnp.float32) + hidden_sum).astype(jnp.bfloat16)
     expanded = jnp.dot(coarse_out, expand_full, preferred_element_type=jnp.float32)
     expanded = expanded.astype(jnp.bfloat16).reshape(
@@ -222,24 +255,22 @@
         coarse_count, width
     )
     delta_out_part = jnp.dot(delta_expand, expand_full.T, preferred_element_type=jnp.float32)
-    delta_coarse_out = lax.psum(delta_out_part.astype(jnp.bfloat16), "mp")
+    delta_coarse_out = sum_all(delta_out_part.astype(jnp.bfloat16), "mp")
     delta_active = jnp.dot(delta_coarse_out, outer_full.T, preferred_element_type=jnp.float32)
     delta_inner = activate_pull(delta_active.astype(jnp.bfloat16))[0]
     delta_norm_part = jnp.dot(delta_inner, inner_full.T, preferred_element_type=jnp.float32)
-    delta_norm = lax.psum(delta_norm_part.astype(jnp.bfloat16), "mp")
+    delta_norm = sum_all(delta_norm_part.astype(jnp.bfloat16), "mp")
     delta_coarse = (
         delta_coarse_out.astype(jnp.float32) + coarse_pull(delta_norm)[0].astype(jnp.float32)
     ).astype(jnp.bfloat16)
     delta_columns = lax.dynamic_slice_in_dim(
-        delta_coarse, processor_position * stripe_span, stripe_span, 1
+        turn(delta_coarse, lon_count, lon_here), processor_position * stripe_span, stripe_span, 1
     )
     delta_merge_part = jnp.dot(delta_columns, merge_full.T, preferred_element_type=jnp.float32)
-    delta_merge_part = delta_merge_part.reshape(
+    delta_merge_part = turn(delta_merge_part.astype(jnp.bfloat16), lon_count, lon_here).reshape(
         levels, row_count // 2, column_count // 2, 4 * width
     )
-    delta_merged = lax.psum_scatter(
-        delta_merge_part.astype(jnp.bfloat16), "mp", scatter_dimension=2, tiled=True
-    )
+    delta_merged = sum_scatter(columns_first(delta_merge_part), "mp").astype(jnp.bfloat16)
     delta_hidden_merge = merge_pull(delta_merged)[0]
     delta_hidden = (
         result_gradient.astype(jnp.float32) + delta_hidden_merge.astype(jnp.float32)
@@ -252,7 +283,9 @@
     delta_mixed = roll_ahead(delta_mixed_back)
     delta_stacked = attend_pull(delta_mixed)[0]
     delta_normed_part = jnp.dot(delta_stacked, joined.T, preferred_element_type=jnp.float32)
-    delta_normed = lax.psum(delta_normed_part.astype(jnp.bfloat16), "mp")
+    delta_normed = sum_all(
+        delta_normed_part.astype(jnp.bfloat16).reshape(-1, width), "mp"
+    ).reshape(delta_normed_part.shape)
     delta_source = norm_pull(delta_normed)[0]
     delta_source = roll_back(delta_source)
     own_delta = lax.dynamic_slice_in_dim(

time: 327 us -> 305 us (0.933)
  waiting for transfers between devices: 212 us -> 70.3 us
  starting transfers between devices: 16.4 us -> 64.3 us
  local copies, waits for them, and re-layouts: 11.8 us -> 52.3 us
  blocking collectives: 33.2 us -> 60.9 us
  other arithmetic: 17.2 us -> 24.9 us
  between operations: 17 us -> 9.56 us
    all_gather x4 -> x0, waiting for transfers between devices: 83.4 us -> none  [the longest x1 44.4 us: per_device(): lax.all_gather(shrunk_dense_second, 'lon', axis=1, tiled=True)]
    psum x3 -> x0, waiting for transfers between devices: 66.6 us -> none  [the longest x1 36.4 us: per_device(): hidden_sum = lax.psum(outer.astype(jnp.bfloat16), 'mp').astype(jnp.float32)]
    ppermute x8 -> x20, waiting for transfers between devices: 21.1 us -> 57 us  [shifted(): lax.ppermute(value, axis, [(i, (i + by) % devices) for i in range(devices)])]
    all_gather x0 -> x4, blocking collectives: none -> 34.6 us  [sum_all(): return lax.all_gather(own.astype(value.dtype), axis, axis=0, tiled=True)]
    unnamed x10 -> x0, waiting for transfers between devices: 32.3 us -> none
    all_to_all x0 -> x7, starting transfers between devices: none -> 25 us  [the longest x6 21.6 us: sum_scatter(): moved = lax.all_to_all(value, axis, split_axis=0, concat_axis=0, tiled=True)]
    ppermute x8 -> x20, starting transfers between devices: 16 us -> 39.4 us  [shifted(): lax.ppermute(value, axis, [(i, (i + by) % devices) for i in range(devices)])]
    unnamed x68 -> x116, local copies, waits for them, and re-layouts: 3.17 us -> 20.3 us
  transfers between devices with their start and end apart: 17 -> 27, of which waited for: 14 -> 11; matrix products, arithmetic and copies ran while one was open for 7% -> 17% of each run, Pallas kernels for 0% -> 0%
where the time goes in v1:
time: 305 us; the launch traced here: 303 us
  waiting for transfers between devices  70.3 us (23%)
  starting transfers between devices  64.3 us (21%)
  blocking collectives  60.9 us (20%)
  local copies, waits for them, and re-layouts  52.3 us (17%)
  other arithmetic  24.9 us (8%)
  matrix products  20.8 us (7%)
  between operations  9.56 us (3%)
    ppermute x20, waiting for transfers between devices, shifted(): lax.ppermute(value, axis, [(i, (i + by) % devices) for i in range(devices)])  57 us
    ppermute x20, starting transfers between devices, shifted(): lax.ppermute(value, axis, [(i, (i + by) % devices) for i in range(devices)])  39.4 us
    all_gather x4, blocking collectives, sum_all(): return lax.all_gather(own.astype(value.dtype), axis, axis=0, tiled=True)  34.6 us
    all_to_all x6, starting transfers between devices, sum_scatter(): moved = lax.all_to_all(value, axis, split_axis=0, concat_axis=0, tiled=True)  21.6 us
    unnamed x116, local copies, waits for them, and re-layouts  20.3 us
    all_to_all x6, waiting for transfers between devices, sum_scatter(): moved = lax.all_to_all(value, axis, split_axis=0, concat_axis=0, tiled=True)  13.3 us
    all_to_all x1, blocking collectives, per_device(): lax.all_to_all(expanded, 'mp', split_axis=2, concat_axis=3, tiled=True)  6.99 us
    all_gather x1, blocking collectives, per_device(): gathered_in = lax.all_gather(merged_in, 'mp', axis=2, tiled=True)  6.77 us
  transfers between devices with their start and end apart: 27, of which 11 were waited for; matrix products, arithmetic and copies ran while one was open for 17% of the time, Pallas kernels for 0%

profile of v1, /device:TPU:0, one launch (start us, length us, event | category | flops | bytes accessed | tf_op | source)
XLA Modules:
  0.0 303.1 jit_solution(2837687228328558570)
XLA Ops:
  34.1 3.7 %collective-permute-done.1 = bf16[2,16,4,512]{3,2,1,0:T(4,128)(2,1)S(1)} collective-permute-done((bf16[2,16,4,512]{3,2,1,0:T(4,128)(2,1)S(1)}, bf16[2,16,4,512]{3,2,1,0:T(4,128)(2,1)S(1)}, u32[]{:S(2)}, u32[]{:S(2)}) %collective-permute-start.1) | collective-permute-done | bytes 131104 | tf_op jit(solution)/shard_map/ppermute | solution.py:14
  37.8 5.0 %collective-permute-start.11 = (bf16[1024,256]{1,0:T(8,128)(2,1)}, bf16[1024,256]{1,0:T(8,128)(2,1)}, u32[]{:S(2)}, u32[]{:S(2)}) collective-permute-start(bf16[1024,256]{1,0:T(8,128)(2,1)} %param.17), channel_id=1, source_target_pairs={{0,8},{4,12},{8,0},{12,4},{1,9},{5,13},{9,1},{13,5},{2,10},{6,14},... | collective-permute-start | bytes 1572872 | tf_op jit(solution)/shard_map/ppermute | solution.py:14
  62.1 4.1 %all-to-all-start.4 = ((bf16[4,32,1024]{2,1,0:T(8,128)(2,1)}), bf16[4,32,1024]{2,1,0:T(8,128)(2,1)}, u32[]{:S(2)}, u32[]{:S(2)}) async-start(bf16[4,32,1024]{2,1,0:T(8,128)(2,1)} %bitcast.220), calls=%async_computation.4 | async-start | bytes 524288 | tf_op jit(solution)/shard_map/all_to_all | solution.py:154
  66.2 10.1 %collective-permute-done.4 = bf16[512,256]{1,0:T(8,128)(2,1)} collective-permute-done((bf16[512,256]{1,0:T(8,128)(2,1)}, bf16[512,256]{1,0:T(8,128)(2,1)}, u32[]{:S(2)}, u32[]{:S(2)}) %collective-permute-start.4) | collective-permute-done | bytes 262176 | tf_op jit(solution)/shard_map/ppermute | solution.py:14
  78.0 16.6 %collective-permute-done.5 = bf16[512,256]{1,0:T(8,128)(2,1)} collective-permute-done((bf16[512,256]{1,0:T(8,128)(2,1)}, bf16[512,256]{1,0:T(8,128)(2,1)}, u32[]{:S(2)}, u32[]{:S(2)}) %collective-permute-start.5) | collective-permute-done | bytes 262176 | tf_op jit(solution)/shard_map/ppermute | solution.py:14
  94.6 6.2 %collective-permute-start.2 = (bf16[2,16,4,128]{3,2,1,0:T(4,128)(2,1)S(1)}, bf16[2,16,4,128]{3,2,1,0:T(4,128)(2,1)S(1)}, u32[]{:S(2)}, u32[]{:S(2)}) collective-permute-start(bf16[2,16,4,128]{3,2,1,0:T(4,128)(2,1)S(1)} %slice.109), channel_id=1, source_target_pairs={{0,4},{4,8},{8,12},{12,0},{1,5},{5,9},{9,13},{13,1},{2,6},{6,10},{... | collective-permute-start | bytes 98312 | tf_op jit(solution)/shard_map/ppermute | solution.py:14
  101.8 3.7 %collective-permute-done.2 = bf16[2,16,4,128]{3,2,1,0:T(4,128)(2,1)S(1)} collective-permute-done((bf16[2,16,4,128]{3,2,1,0:T(4,128)(2,1)S(1)}, bf16[2,16,4,128]{3,2,1,0:T(4,128)(2,1)S(1)}, u32[]{:S(2)}, u32[]{:S(2)}) %collective-permute-start.2) | collective-permute-done | bytes 32800 | tf_op jit(solution)/shard_map/ppermute | solution.py:14
  118.1 10.5 %all_gather.24 = bf16[128,1024]{1,0:T(8,128)(2,1)} all-gather(bf16[32,1024]{1,0:T(8,128)(2,1)S(1)} %reduce_sum.280), channel_id=1, replica_groups=mesh['lat'=2,'lon'=4,'mp'=4] {'mp'}, dimensions={0}, use_global_device_ids=true | all-gather | bytes 327680 | tf_op jit(solution)/shard_map/all_gather | solution.py:162
  137.4 6.0 %collective-permute-done.8 = bf16[256,1024]{1,0:T(8,128)(2,1)} collective-permute-done((bf16[256,1024]{1,0:T(8,128)(2,1)}, bf16[256,1024]{1,0:T(8,128)(2,1)}, u32[]{:S(2)}, u32[]{:S(2)}) %collective-permute-start.8) | collective-permute-done | bytes 524320 | tf_op jit(solution)/shard_map/ppermute | solution.py:14
  145.3 8.8 %collective-permute-done.9 = bf16[256,1024]{1,0:T(8,128)(2,1)S(1)} collective-permute-done((bf16[256,1024]{1,0:T(8,128)(2,1)}, bf16[256,1024]{1,0:T(8,128)(2,1)S(1)}, u32[]{:S(2)}, u32[]{:S(2)}) %collective-permute-start.9) | collective-permute-done | bytes 524320 | tf_op jit(solution)/shard_map/ppermute | solution.py:14
  158.0 6.8 %all_gather.21 = bf16[2,8,8,2048]{3,1,2,0:T(8,128)(2,1)S(1)} all-gather(bf16[2,8,2,2048]{3,1,2,0:T(8,128)(2,1)S(1)} %multiply_convert_fusion.4), channel_id=1, replica_groups=mesh['lat'=2,'lon'=4,'mp'=4] {'mp'}, dimensions={2}, use_global_device_ids=true | all-gather | bytes 655360 | tf_op jit(solution)/shard_map/all_gather | solution.py:218
  168.9 6.0 %all_gather.22 = bf16[128,1024]{1,0:T(8,128)(2,1)S(1)} all-gather(bf16[128,256]{1,0:T(8,128)(2,1)S(1)} %convolution_convert_fusion.16), channel_id=1, replica_groups=mesh['lat'=2,'lon'=4,'mp'=4] {'mp'}, dimensions={1}, use_global_device_ids=true | all-gather | bytes 327680 | tf_op jit(solution)/shard_map/all_gather | solution.py:228
  179.0 4.8 %convolution_convert_fusion.5 = bf16[128,1024]{1,0:T(8,128)(2,1)} fusion(bf16[1024,1024]{1,0:T(8,128)(2,1)} %constant_dynamic-update-slice_fusion.4, f32[128,1024]{1,0:T(8,128)} %fusion.2, bf16[128,1024]{1,0:T(8,128)(2,1)S(1)} %copy-done.4, bf16[1024,1024]{1,0:T(8,128)(2,1)} %constant_dynamic-update-slice_fusion.8), kind=kOutput, calls=%fused_computation.9 | convolution fusion | flops 539885568 | bytes 5242880 | tf_op jit(solution)/shard_map/dot_general | solution.py:261
  187.2 6.0 %all-to-all-done.5 = bf16[4,32,1024]{2,1,0:T(8,128)(2,1)S(1)} async-done(((bf16[4,32,1024]{2,1,0:T(8,128)(2,1)}), bf16[4,32,1024]{2,1,0:T(8,128)(2,1)S(1)}, u32[]{:S(2)}, u32[]{:S(2)}) %all-to-all-start.5) | async-done | bytes 262176 | tf_op jit(solution)/shard_map/all_to_all | solution.py:154
  193.9 6.0 %all_gather.25 = bf16[128,1024]{1,0:T(8,128)(2,1)S(1)} all-gather(bf16[32,1024]{1,0:T(8,128)(2,1)} %reduce_sum.281), channel_id=1, replica_groups=mesh['lat'=2,'lon'=4,'mp'=4] {'mp'}, dimensions={0}, use_global_device_ids=true | all-gather | bytes 327680 | tf_op jit(solution)/shard_map/all_gather | solution.py:162
  209.2 3.9 %dynamic-slice_reduce_fusion.3 = (bf16[128,512]{1,0:T(8,128)(2,1)}, bf16[128,512]{1,0:T(8,128)(2,1)}, bf16[128,512]{1,0:T(8,128)(2,1)}, bf16[128,512]{1,0:T(8,128)(2,1)}) fusion(bf16[128,4,512]{2,1,0:T(4,128)(2,1)S(1)} %reshape.312, s32[]{:T(128)S(6)} %select_n.85, s32[]{:T(128)S(6)} %select_n.87, s32[]{:T(128)S(6)} %select_n.86, s32[]{:T(128)S(6)} %select_n.88), kind=kLoop, calls=%fused_computation.124 | loop fusion | bytes 1048592 | tf_op jit(solution)/shard_map/jit(dynamic_index_in_dim)/dynamic_slice | solution.py:149
  218.7 3.7 %all-to-all-start.6 = ((bf16[4,2,8,2,2048]{4,3,2,1,0:T(2,128)(2,1)}), bf16[4,2,8,2,2048]{4,3,2,1,0:T(2,128)(2,1)S(1)}, u32[]{:S(2)}, u32[]{:S(2)}) async-start(bf16[4,2,8,2,2048]{4,3,2,1,0:T(2,128)(2,1)} %copy.240), calls=%async_computation.6 | async-start | bytes 1048576 | tf_op jit(solution)/shard_map/all_to_all | solution.py:154
  223.7 7.3 %all-to-all-done.6 = bf16[4,2,8,2,2048]{4,3,2,1,0:T(2,128)(2,1)S(1)} async-done(((bf16[4,2,8,2,2048]{4,3,2,1,0:T(2,128)(2,1)}), bf16[4,2,8,2,2048]{4,3,2,1,0:T(2,128)(2,1)S(1)}, u32[]{:S(2)}, u32[]{:S(2)}) %all-to-all-start.6) | async-done | bytes 524320 | tf_op jit(solution)/shard_map/all_to_all | solution.py:154
  237.9 6.5 %all_gather.26 = bf16[2,16,16,512]{3,1,0,2:T(8,128)(2,1)S(1)} all-gather(bf16[2,16,4,512]{3,1,0,2:T(8,128)(2,1)S(1)} %copy.246), channel_id=1, replica_groups=mesh['lat'=2,'lon'=4,'mp'=4] {'mp'}, dimensions={2}, use_global_device_ids=true | all-gather | bytes 655360 | tf_op jit(solution)/shard_map/all_gather | solution.py:279
  263.0 3.6 %all-to-all-start.7 = ((bf16[4,128,512]{2,1,0:T(8,128)(2,1)}), bf16[4,128,512]{2,1,0:T(8,128)(2,1)S(1)}, u32[]{:S(2)}, u32[]{:S(2)}) async-start(bf16[4,128,512]{2,1,0:T(8,128)(2,1)} %bitcast.65), calls=%async_computation.7 | async-start | bytes 1048576 | tf_op jit(solution)/shard_map/all_to_all | solution.py:154
  266.8 10.9 %all_gather.23 = bf16[128,1024]{1,0:T(8,128)(2,1)S(1)} all-gather(bf16[32,1024]{1,0:T(8,128)(2,1)S(1)} %reduce_sum.279), channel_id=1, replica_groups=mesh['lat'=2,'lon'=4,'mp'=4] {'mp'}, dimensions={0}, use_global_device_ids=true | all-gather | bytes 327680 | tf_op jit(solution)/shard_map/all_gather | solution.py:162
  277.7 7.3 %all_gather.27 = bf16[512,512]{1,0:T(8,128)(2,1)S(1)} all-gather(bf16[128,512]{1,0:T(8,128)(2,1)S(1)} %reduce_sum.290), channel_id=1, replica_groups=mesh['lat'=2,'lon'=4,'mp'=4] {'mp'}, dimensions={0}, use_global_device_ids=true | all-gather | bytes 655360 | tf_op jit(solution)/shard_map/all_gather | solution.py:162
  289.9 7.0 %all_to_all.57 = bf16[2,8,8,1,512]{4,1,0,3,2:T(8,128)(2,1)S(1)} all-to-all(bf16[2,8,8,1,512]{4,1,0,3,2:T(8,128)(2,1)S(1)} %copy.223), channel_id=1, replica_groups=mesh['lat'=2,'lon'=4,'mp'=4] {'mp'}, dimensions={2} | all-to-all | bytes 262144 | tf_op jit(solution)/shard_map/all_to_all | solution.py:240
  298.5 3.7 %collective-permute-done.19 = bf16[2,4,16,512]{3,2,1,0:T(8,128)(2,1)S(1)} collective-permute-done((bf16[2,4,16,512]{3,2,1,0:T(8,128)(2,1)S(1)}, bf16[2,4,16,512]{3,2,1,0:T(8,128)(2,1)S(1)}, u32[]{:S(2)}, u32[]{:S(2)}) %collective-permute-start.19) | collective-permute-done | bytes 131104 | tf_op jit(solution)/shard_map/ppermute | solution.py:14
  (303 shorter events, 135.7 us)
Async XLA Ops:
  0.7 45.9 %collective-permute-start.13 = (bf16[256,512]{1,0:T(8,128)(2,1)}, bf16[256,512]{1,0:T(8,128)(2,1)}, u32[]{:S(2)}, u32[]{:S(2)}) collective-permute-start(bf16[256,512]{1,0:T(8,128)(2,1)} %param.18), channel_id=1, source_target_pairs={{0,4},{4,8},{8,12},{12,0},{1,5},{5,9},{9,13},{13,1},{2,6},{6,10},{... | collective-permute-start | bytes 786440 | tf_op jit(solution)/shard_map/ppermute | solution.py:14
  3.8 48.1 %collective-permute-start.14 = (bf16[256,512]{1,0:T(8,128)(2,1)}, bf16[256,512]{1,0:T(8,128)(2,1)}, u32[]{:S(2)}, u32[]{:S(2)}) collective-permute-start(bf16[256,512]{1,0:T(8,128)(2,1)} %param.18), channel_id=1, source_target_pairs={{0,8},{4,12},{8,0},{12,4},{1,9},{5,13},{9,1},{13,5},{2,10},{6,14},... | collective-permute-start | bytes 786440 | tf_op jit(solution)/shard_map/ppermute | solution.py:14
  6.4 48.2 %collective-permute-start.15 = (bf16[256,512]{1,0:T(8,128)(2,1)}, bf16[256,512]{1,0:T(8,128)(2,1)}, u32[]{:S(2)}, u32[]{:S(2)}) collective-permute-start(bf16[256,512]{1,0:T(8,128)(2,1)} %param.18), channel_id=1, source_target_pairs={{0,12},{4,0},{8,4},{12,8},{1,13},{5,1},{9,5},{13,9},{2,14},{6,2},{... | collective-permute-start | bytes 786440 | tf_op jit(solution)/shard_map/ppermute | solution.py:14
  8.6 12.8 %collective-permute-start = (bf16[2,4,16,512]{3,2,1,0:T(8,128)(2,1)S(1)}, bf16[2,4,16,512]{3,2,1,0:T(8,128)(2,1)S(1)}, u32[]{:S(2)}, u32[]{:S(2)}) collective-permute-start(bf16[2,4,16,512]{3,2,1,0:T(8,128)(2,1)S(1)} %slice.82), channel_id=1, source_target_pairs={{0,16},{16,0},{1,17},{17,1},{2,18},{18,2},{3,19},{19,3},{4,20},{20... | collective-permute-start | bytes 393224 | tf_op jit(solution)/shard_map/ppermute | solution.py:14
  10.2 118.3 %collective-permute-start.10 = (bf16[1024,256]{1,0:T(8,128)(2,1)}, bf16[1024,256]{1,0:T(8,128)(2,1)}, u32[]{:S(2)}, u32[]{:S(2)}) collective-permute-start(bf16[1024,256]{1,0:T(8,128)(2,1)} %param.17), channel_id=1, source_target_pairs={{0,4},{4,8},{8,12},{12,0},{1,5},{5,9},{9,13},{13,1},{2,6},{6,10},{... | collective-permute-start | bytes 1572872 | tf_op jit(solution)/shard_map/ppermute | solution.py:14
  12.7 20.5 %all-to-all-start.3 = ((bf16[2,8,2,4,512]{4,1,2,0,3:T(8,128)(2,1)}), bf16[2,8,2,4,512]{4,1,2,0,3:T(8,128)(2,1)S(1)}, u32[]{:S(2)}, u32[]{:S(2)}) async-start(bf16[2,8,2,4,512]{4,1,2,0,3:T(8,128)(2,1)} %bitcast.38), calls=%async_computation.3 | async-start | bytes 262144 | tf_op jit(solution)/shard_map/all_to_all | solution.py:254
  21.5 16.3 %collective-permute-start.1 = (bf16[2,16,4,512]{3,2,1,0:T(4,128)(2,1)S(1)}, bf16[2,16,4,512]{3,2,1,0:T(4,128)(2,1)S(1)}, u32[]{:S(2)}, u32[]{:S(2)}) collective-permute-start(bf16[2,16,4,512]{3,2,1,0:T(4,128)(2,1)S(1)} %pad_maximum_fusion.4), channel_id=1, source_target_pairs={{0,12},{4,0},{8,4},{12,8},{1,13},{5,1},{9,5},{13,9},{2,14},{6,2},{... | collective-permute-start | bytes 393224 | tf_op jit(solution)/shard_map/ppermute | solution.py:14
  37.8 93.9 %collective-permute-start.11 = (bf16[1024,256]{1,0:T(8,128)(2,1)}, bf16[1024,256]{1,0:T(8,128)(2,1)}, u32[]{:S(2)}, u32[]{:S(2)}) collective-permute-start(bf16[1024,256]{1,0:T(8,128)(2,1)} %param.17), channel_id=1, source_target_pairs={{0,8},{4,12},{8,0},{12,4},{1,9},{5,13},{9,1},{13,5},{2,10},{6,14},... | collective-permute-start | bytes 1572872 | tf_op jit(solution)/shard_map/ppermute | solution.py:14
  46.6 87.0 %collective-permute-start.12 = (bf16[1024,256]{1,0:T(8,128)(2,1)}, bf16[1024,256]{1,0:T(8,128)(2,1)}, u32[]{:S(2)}, u32[]{:S(2)}) collective-permute-start(bf16[1024,256]{1,0:T(8,128)(2,1)} %param.17), channel_id=1, source_target_pairs={{0,12},{4,0},{8,4},{12,8},{1,13},{5,1},{9,5},{13,9},{2,14},{6,2},{... | collective-permute-start | bytes 1572872 | tf_op jit(solution)/shard_map/ppermute | solution.py:14
  51.8 24.4 %collective-permute-start.4 = (bf16[512,256]{1,0:T(8,128)(2,1)}, bf16[512,256]{1,0:T(8,128)(2,1)}, u32[]{:S(2)}, u32[]{:S(2)}) collective-permute-start(bf16[512,256]{1,0:T(8,128)(2,1)} %param.15), channel_id=1, source_target_pairs={{0,4},{4,8},{8,12},{12,0},{1,5},{5,9},{9,13},{13,1},{2,6},{6,10},{... | collective-permute-start | bytes 786440 | tf_op jit(solution)/shard_map/ppermute | solution.py:14
  54.6 40.0 %collective-permute-start.5 = (bf16[512,256]{1,0:T(8,128)(2,1)}, bf16[512,256]{1,0:T(8,128)(2,1)}, u32[]{:S(2)}, u32[]{:S(2)}) collective-permute-start(bf16[512,256]{1,0:T(8,128)(2,1)} %param.15), channel_id=1, source_target_pairs={{0,8},{4,12},{8,0},{12,4},{1,9},{5,13},{9,1},{13,5},{2,10},{6,14},... | collective-permute-start | bytes 786440 | tf_op jit(solution)/shard_map/ppermute | solution.py:14
  62.1 51.5 %all-to-all-start.4 = ((bf16[4,32,1024]{2,1,0:T(8,128)(2,1)}), bf16[4,32,1024]{2,1,0:T(8,128)(2,1)}, u32[]{:S(2)}, u32[]{:S(2)}) async-start(bf16[4,32,1024]{2,1,0:T(8,128)(2,1)} %bitcast.220), calls=%async_computation.4 | async-start | bytes 524288 | tf_op jit(solution)/shard_map/all_to_all | solution.py:154
  76.3 29.2 %collective-permute-start.6 = (bf16[512,256]{1,0:T(8,128)(2,1)}, bf16[512,256]{1,0:T(8,128)(2,1)S(1)}, u32[]{:S(2)}, u32[]{:S(2)}) collective-permute-start(bf16[512,256]{1,0:T(8,128)(2,1)} %param.15), channel_id=1, source_target_pairs={{0,12},{4,0},{8,4},{12,8},{1,13},{5,1},{9,5},{13,9},{2,14},{6,2},{... | collective-permute-start | bytes 786440 | tf_op jit(solution)/shard_map/ppermute | solution.py:14
  94.6 10.9 %collective-permute-start.2 = (bf16[2,16,4,128]{3,2,1,0:T(4,128)(2,1)S(1)}, bf16[2,16,4,128]{3,2,1,0:T(4,128)(2,1)S(1)}, u32[]{:S(2)}, u32[]{:S(2)}) collective-permute-start(bf16[2,16,4,128]{3,2,1,0:T(4,128)(2,1)S(1)} %slice.109), channel_id=1, source_target_pairs={{0,4},{4,8},{8,12},{12,0},{1,5},{5,9},{9,13},{13,1},{2,6},{6,10},{... | collective-permute-start | bytes 98312 | tf_op jit(solution)/shard_map/ppermute | solution.py:14
  105.5 30.0 %collective-permute-start.7 = (bf16[256,1024]{1,0:T(8,128)(2,1)}, bf16[256,1024]{1,0:T(8,128)(2,1)}, u32[]{:S(2)}, u32[]{:S(2)}) collective-permute-start(bf16[256,1024]{1,0:T(8,128)(2,1)} %param.16), channel_id=1, source_target_pairs={{0,4},{4,8},{8,12},{12,0},{1,5},{5,9},{9,13},{13,1},{2,6},{6,10},{... | collective-permute-start | bytes 1572872 | tf_op jit(solution)/shard_map/ppermute | solution.py:14
  109.5 33.9 %collective-permute-start.8 = (bf16[256,1024]{1,0:T(8,128)(2,1)}, bf16[256,1024]{1,0:T(8,128)(2,1)}, u32[]{:S(2)}, u32[]{:S(2)}) collective-permute-start(bf16[256,1024]{1,0:T(8,128)(2,1)} %param.16), channel_id=1, source_target_pairs={{0,8},{4,12},{8,0},{12,4},{1,9},{5,13},{9,1},{13,5},{2,10},{6,14},... | collective-permute-start | bytes 1572872 | tf_op jit(solution)/shard_map/ppermute | solution.py:14
  113.6 41.3 %all-to-all-start = ((bf16[4,2,16,4,512]{4,3,2,1,0:T(4,128)(2,1)}), bf16[4,2,16,4,512]{4,3,2,1,0:T(4,128)(2,1)S(1)}, u32[]{:S(2)}, u32[]{:S(2)}) async-start(bf16[4,2,16,4,512]{4,3,2,1,0:T(4,128)(2,1)} %bitcast.153), calls=%async_computation | async-start | bytes 1048576 | tf_op jit(solution)/shard_map/all_to_all | solution.py:154
  128.5 25.5 %collective-permute-start.9 = (bf16[256,1024]{1,0:T(8,128)(2,1)}, bf16[256,1024]{1,0:T(8,128)(2,1)S(1)}, u32[]{:S(2)}, u32[]{:S(2)}) collective-permute-start(bf16[256,1024]{1,0:T(8,128)(2,1)} %param.16), channel_id=1, source_target_pairs={{0,12},{4,0},{8,4},{12,8},{1,13},{5,1},{9,5},{13,9},{2,14},{6,2},{... | collective-permute-start | bytes 1572872 | tf_op jit(solution)/shard_map/ppermute | solution.py:14
  183.8 9.4 %all-to-all-start.5 = ((bf16[4,32,1024]{2,1,0:T(8,128)(2,1)}), bf16[4,32,1024]{2,1,0:T(8,128)(2,1)S(1)}, u32[]{:S(2)}, u32[]{:S(2)}) async-start(bf16[4,32,1024]{2,1,0:T(8,128)(2,1)} %bitcast.244), calls=%async_computation.5 | async-start | bytes 524288 | tf_op jit(solution)/shard_map/all_to_all | solution.py:154
  218.7 12.3 %all-to-all-start.6 = ((bf16[4,2,8,2,2048]{4,3,2,1,0:T(2,128)(2,1)}), bf16[4,2,8,2,2048]{4,3,2,1,0:T(2,128)(2,1)S(1)}, u32[]{:S(2)}, u32[]{:S(2)}) async-start(bf16[4,2,8,2,2048]{4,3,2,1,0:T(2,128)(2,1)} %copy.240), calls=%async_computation.6 | async-start | bytes 1048576 | tf_op jit(solution)/shard_map/all_to_all | solution.py:154
  244.8 7.1 %collective-permute-start.16 = (bf16[2,4,16,128]{3,2,1,0:T(8,128)(2,1)S(1)}, bf16[2,4,16,128]{3,2,1,0:T(8,128)(2,1)S(1)}, u32[]{:S(2)}, u32[]{:S(2)}) collective-permute-start(bf16[2,4,16,128]{3,2,1,0:T(8,128)(2,1)S(1)} %slice.112), channel_id=1, source_target_pairs={{0,16},{16,0},{1,17},{17,1},{2,18},{18,2},{3,19},{19,3},{4,20},{20... | collective-permute-start | bytes 98312 | tf_op jit(solution)/shard_map/ppermute | solution.py:14
  247.6 15.4 %all-to-all-start.1 = ((bf16[4,32,1024]{2,1,0:T(8,128)(2,1)}), bf16[4,32,1024]{2,1,0:T(8,128)(2,1)S(1)}, u32[]{:S(2)}, u32[]{:S(2)}) async-start(bf16[4,32,1024]{2,1,0:T(8,128)(2,1)} %bitcast.27), calls=%async_computation.1 | async-start | bytes 524288 | tf_op jit(solution)/shard_map/all_to_all | solution.py:154
  263.0 14.6 %all-to-all-start.7 = ((bf16[4,128,512]{2,1,0:T(8,128)(2,1)}), bf16[4,128,512]{2,1,0:T(8,128)(2,1)S(1)}, u32[]{:S(2)}, u32[]{:S(2)}) async-start(bf16[4,128,512]{2,1,0:T(8,128)(2,1)} %bitcast.65), calls=%async_computation.7 | async-start | bytes 1048576 | tf_op jit(solution)/shard_map/all_to_all | solution.py:154
  286.9 10.3 %collective-permute-start.18 = (bf16[2,16,4,512]{3,2,1,0:T(4,128)(2,1)S(1)}, bf16[2,16,4,512]{3,2,1,0:T(4,128)(2,1)S(1)}, u32[]{:S(2)}, u32[]{:S(2)}) collective-permute-start(bf16[2,16,4,512]{3,2,1,0:T(4,128)(2,1)S(1)} %slice.115), channel_id=1, source_target_pairs={{0,4},{4,8},{8,12},{12,0},{1,5},{5,9},{9,13},{13,1},{2,6},{6,10},{... | collective-permute-start | bytes 393224 | tf_op jit(solution)/shard_map/ppermute | solution.py:14
  (49 other events, 448.5 us)

commit v2 on v0

v2 whole, which is shorter than its diff:
```python
import functools
import jax
import jax.numpy as jnp
from jax import lax
from jax.experimental import pallas as pl
from jax.experimental.pallas import tpu as pltpu
from jax.sharding import PartitionSpec as P

TILE_SIDE_CELLS = 8
HALF = TILE_SIDE_CELLS // 2

epsilon = 1e-05
bf16 = jnp.bfloat16
f32 = jnp.float32


def dot(a, b, ca=1, cb=0):
    return lax.dot_general(a, b, (((ca,), (cb,)), ((), ())), preferred_element_type=f32)


def norm_parts(values, axes):
    center = values - jnp.mean(values, axes, keepdims=True)
    spread = jnp.mean(center * center, axes, keepdims=True)
    scale = lax.rsqrt(spread + epsilon)
    return center * scale, scale


def norm_back(delta, normal, scale, axes):
    return scale * (
        delta
        - jnp.mean(delta, axes, keepdims=True)
        - normal * jnp.mean(delta * normal, axes, keepdims=True)
    )


GELU_A = 0.7978845608028654
GELU_B = 0.044715


def gelu(x):
    return 0.5 * x * (1.0 + jnp.tanh(GELU_A * (x + GELU_B * x * x * x)))


def gelu_back(x):
    t = jnp.tanh(GELU_A * (x + GELU_B * x * x * x))
    return 0.5 * (1.0 + t) + 0.5 * x * (1.0 - t * t) * GELU_A * (1.0 + 3.0 * GELU_B * x * x)


def unit(values):
    length = jnp.sqrt(jnp.sum(values * values, -1, keepdims=True))
    return values / jnp.maximum(length, 1.0)


def unit_back(delta, values):
    length = jnp.sqrt(jnp.sum(values * values, -1, keepdims=True))
    inverse = 1.0 / jnp.maximum(length, 1.0)
    share = jnp.where(length > 1.0, 1.0, jnp.where(length == 1.0, 0.5, 0.0))
    along = jnp.sum(delta * values, -1, keepdims=True)
    return delta * inverse - share * values * (along * inverse * inverse * inverse)


def kernel(
    sizes,
    x_ref,
    joined_ref,
    out_weight_ref,
    scale_ref,
    merge_ref,
    first_ref,
    second_ref,
    unfold_ref,
    g_ref,
    output_ref,
    grad_ref,
    xe,
    me,
    de,
    le,
    wm,
    wf,
    ws,
    wu,
    stacked_ref,
    probs_ref,
    attn_back,
    send_a,
    recv_a,
    merged_all,
    columns_all,
    send_o,
    recv_o,
    out_all,
    send_e,
    recv_e,
    delta_e,
    send_d,
    recv_d,
    delta_all,
    send_n,
    recv_n,
    send_c,
    columns_delta,
    send_m,
    recv_m,
    hidden_all,
    send_l,
    recv_l,
    send_sem,
    recv_sem,
    local_sem,
):
    n_lat, n_lon, n_mp, nbi, nbj, cells = sizes
    width = x_ref.shape[-1]
    la, lo, p = lax.axis_index("lat"), lax.axis_index("lon"), lax.axis_index("mp")
    rows_q = 4 * nbi * cells
    coarse_q = nbi * cells
    nwi, nwj = nbi // 2, nbj // 2
    window = 4 * 4 * cells
    split = 2 if n_lat == 2 else 1

    def plus(dlat, dlon, dmp):
        return {
            "lat": lax.rem(la + dlat + n_lat, n_lat),
            "lon": lax.rem(lo + dlon + n_lon, n_lon),
            "mp": lax.rem(p + dmp + n_mp, n_mp),
        }

    partners = set()
    for dlat, dlon in ((1, 0), (0, 1), (1, 1)):
        for sign in (1, -1):
            partners.add((sign * dlat % n_lat, sign * dlon % n_lon, 0))
    for by in range(1, n_lon):
        partners.add((0, by, 0))
    for by in range(1, n_mp):
        partners.add((0, 0, by))
    partners = sorted(partners)
    barrier = pltpu.get_barrier_semaphore()
    for offset in partners:
        pl.semaphore_signal(
            barrier, inc=1, device_id=plus(*offset), device_id_type=pl.DeviceIdType.MESH
        )
    pl.semaphore_wait(barrier, len(partners))

    count = [0]
    sent = []

    def send(src, dst, device):
        i = count[0]
        count[0] += 1
        copy = pltpu.make_async_remote_copy(
            src_ref=src,
            dst_ref=dst,
            send_sem=send_sem.at[i],
            recv_sem=recv_sem.at[i],
            device_id=device,
            device_id_type=pl.DeviceIdType.MESH,
        )
        copy.start()
        sent.append(copy)
        return copy

    def arrive(copies):
        for copy in copies:
            copy.wait_recv()

    def to_peers(src_of, dst):
        copies = []
        for by in range(1, n_mp):
            device = plus(0, 0, by)
            copies.append(send(src_of(device["mp"]), dst.at[p], device))
        return copies

    def sum_peers(own, dst):
        total = own.astype(f32)
        for by in range(1, n_mp):
            total = total + dst[lax.rem(p + by, n_mp)].astype(f32)
        return total

    halo = [
        send(x_ref.at[pl.ds(1, nbj - 1), :, 0], xe.at[pl.ds(1, nbj - 1), :, nbi], plus(-1, 0, 0)),
        send(x_ref.at[0, :, pl.ds(1, nbi - 1)], xe.at[nbj, :, pl.ds(1, nbi - 1)], plus(0, -1, 0)),
        send(x_ref.at[0, :, 0], xe.at[nbj, :, nbi], plus(-1, -1, 0)),
    ]
    gradient_moves = to_peers(lambda q: g_ref.at[q], delta_e)

    weights = ((merge_ref, wm), (first_ref, wf), (second_ref, ws), (unfold_ref, wu))
    own_copies = []
    weight_moves = []
    for i, (src, dst) in enumerate(weights):
        part = src.shape[0] // split
        mine = pl.ds(pl.multiple_of(la * part, part) if split > 1 else 0, part)
        copy = pltpu.make_async_copy(src, dst.at[lo], local_sem.at[i])
        copy.start()
        own_copies.append(copy)
        moves = []
        for by in range(1, n_lon):
            moves.append(send(src.at[mine], dst.at[lo, mine], plus(0, by, 0)))
        weight_moves.append((moves, mine))
    across = [None] * len(weights)

    def pass_on(i):
        dst = weights[i][1]
        moves, mine = weight_moves[i]
        across[i] = []
        for by in range(1, n_lon):
            moves[by - 1].wait_recv()
            if split > 1:
                owner = lax.rem(lo - by + n_lon, n_lon)
                across[i].append(send(dst.at[owner, mine], dst.at[owner, mine], plus(1, 0, 0)))

    def ready(i):
        arrive(across[i])
        own_copies[i].wait()

    xe[pl.ds(0, nbj), :, pl.ds(0, nbi)] = x_ref[...]
    arrive(halo)

    def window_blocks(ref):
        parts = []
        for wi in range(nwi):
            for wj in range(nwj):
                for u in range(2):
                    for v in range(2):
                        block = ref[2 * wj + v + 1, :, 2 * wi + u + 1].astype(f32)
                        parts.append(block.reshape(4 * cells, ref.shape[-1]))
        return jnp.concatenate(parts, 0)

    def block_at(index):
        rest, v = divmod(index, 2)
        rest, u = divmod(rest, 2)
        wi, wj = divmod(rest, nwj)
        return 2 * wj + v + 1, 2 * wi + u + 1

    source = window_blocks(xe)
    normed = norm_parts(source, -1)[0].astype(bf16)
    joined = joined_ref[...]
    stacked = dot(normed, joined).astype(bf16)
    stacked_ref[...] = stacked
    local = joined.shape[1] // 3
    heads = scale_ref.shape[0] // n_mp
    head = local // heads
    t_half = lax.broadcasted_iota(jnp.int32, (window, window), 0) // (window // 2)
    s_half = lax.broadcasted_iota(jnp.int32, (window, window), 1) // (window // 2)
    last = (la == n_lat - 1).astype(f32)
    same = (t_half == s_half).astype(f32)
    gate = jnp.maximum(same, 1.0 - last)

    def slices(w, h):
        def part(k):
            at = k * local + h * head
            return stacked_ref[pl.ds(w * window, window), at : at + head].astype(f32)

        return part(0), part(1), part(2)

    mixed_windows = []
    for w in range(nwi * nwj):
        per_head = []
        for h in range(heads):
            query, key, value = slices(w, h)
            scale = scale_ref[p * heads + h]
            scores = scale * dot(unit(query).astype(bf16), unit(key).astype(bf16), 1, 1)
            raw = jnp.exp(scores)
            if w // nwj == nwi - 1:
                raw = raw * gate
            prob = raw / jnp.sum(raw, -1, keepdims=True)
            probs_ref[w * heads + h] = prob
            per_head.append(dot(prob.astype(bf16), value.astype(bf16)))
        mixed_windows.append(jnp.concatenate(per_head, 1))
    mixed = jnp.concatenate(mixed_windows, 0)
    block_rows = 4 * cells
    for index in range(nbi * nbj):
        bj, bi = block_at(index)
        block = mixed[index * block_rows : (index + 1) * block_rows]
        me[bj, :, bi] = block.reshape(4, cells, local).astype(bf16)
    back = [
        send(me.at[pl.ds(1, nbj - 1), :, nbi], me.at[pl.ds(1, nbj - 1), :, 0], plus(1, 0, 0)),
        send(me.at[nbj, :, pl.ds(1, nbi - 1)], me.at[0, :, pl.ds(1, nbi - 1)], plus(0, 1, 0)),
        send(me.at[nbj, :, nbi], me.at[0, :, 0], plus(1, 1, 0)),
    ]
    pass_on(0)
    arrive(back)
    mixed_back = me[pl.ds(0, nbj), :, pl.ds(0, nbi)].astype(f32).reshape(n_mp * rows_q, local)
    partial = dot(mixed_back.astype(bf16), out_weight_ref[...]).astype(bf16)
    send_a[...] = partial.reshape(n_mp, rows_q, width)
    moves = to_peers(lambda q: send_a.at[q], recv_a)
    pass_on(1)
    arrive(moves)
    own_fine = x_ref[p].astype(f32).reshape(rows_q, width)
    hidden = (own_fine + sum_peers(send_a[p], recv_a)).astype(bf16)
    hidden = hidden.astype(f32).reshape(4, coarse_q, width)
    merge_normal, merge_scale = norm_parts(hidden, (0, 2))
    merged_all[p] = merge_normal.astype(bf16)
    moves = to_peers(lambda q: merged_all.at[p], merged_all)
    ready(0)
    merge_full = wm[...].reshape(4 * width, wm.shape[-1])
    arrive(moves)
    columns = jnp.zeros((n_mp * coarse_q, wm.shape[-1]), f32)
    for s in range(4):
        tokens = merged_all[:, s].reshape(n_mp * coarse_q, width)
        columns = columns + dot(tokens, merge_full[s * width : (s + 1) * width])
    columns_all[p] = columns.astype(bf16)
    moves = to_peers(lambda q: columns_all.at[p], columns_all)
    pass_on(2)
    pass_on(3)

    for q in range(n_mp):
        @pl.when(p == q)
        def _(q=q):
            delta_e[q] = g_ref[q]

    arrive(gradient_moves)
    ready(3)
    tokens_delta = delta_e[...].reshape(n_mp * coarse_q, width)
    unfold_full = wu[...].reshape(n_lon * wu.shape[1], width)
    coarse_width = unfold_full.shape[0]
    term = dot(tokens_delta, unfold_full, 1, 1).astype(bf16)
    send_d[...] = term.reshape(n_mp, coarse_q, coarse_width)
    moves_d = to_peers(lambda q: send_d.at[q], recv_d)

    arrive(moves)
    coarse = jnp.concatenate([columns_all[r] for r in range(n_mp)], 1).astype(f32)
    coarse_norm = norm_parts(coarse, -1)[0].astype(bf16)
    ready(1)
    first_full = wf[...].reshape(coarse_width, wf.shape[-1])
    inner = dot(coarse_norm, first_full).astype(bf16).astype(f32)
    activated = gelu(inner).astype(bf16)
    ready(2)
    outer = jnp.concatenate([dot(activated, ws[k]) for k in range(n_lon)], 1).astype(bf16)
    send_o[...] = outer.reshape(n_mp, coarse_q, coarse_width)
    moves_o = to_peers(lambda q: send_o.at[q], recv_o)

    arrive(moves_d)
    delta_own = sum_peers(send_d[p], recv_d).astype(bf16)
    delta_all[p] = delta_own
    moves_d = to_peers(lambda q: delta_all.at[p], delta_all)

    arrive(moves_o)
    own_coarse = jnp.concatenate(
        [columns_all[r, pl.ds(pl.multiple_of(p * coarse_q, coarse_q), coarse_q)] for r in range(n_mp)], 1
    ).astype(f32)
    out_all[p] = (own_coarse + sum_peers(send_o[p], recv_o)).astype(bf16)
    moves_o = to_peers(lambda q: out_all.at[p], out_all)

    arrive(moves_d)
    delta_coarse_out = delta_all[...].reshape(n_mp * coarse_q, coarse_width)
    second_width = ws.shape[-1]
    delta_active = jnp.zeros((n_mp * coarse_q, ws.shape[1]), f32)
    for k in range(n_lon):
        piece = delta_coarse_out[:, k * second_width : (k + 1) * second_width]
        delta_active = delta_active + dot(piece, ws[k], 1, 1)
    delta_inner = (delta_active.astype(bf16).astype(f32) * gelu_back(inner)).astype(bf16)
    term = dot(delta_inner, first_full, 1, 1).astype(bf16)
    send_n[...] = term.reshape(n_mp, coarse_q, coarse_width)
    moves_n = to_peers(lambda q: send_n.at[q], recv_n)

    arrive(moves_o)
    coarse_out = out_all[...].reshape(n_mp * coarse_q, coarse_width)
    send_e[...] = dot(coarse_out, unfold_full).astype(bf16).reshape(n_mp, coarse_q, width)
    moves_e = to_peers(lambda q: send_e.at[q], recv_e)

    arrive(moves_n)
    delta_norm = sum_peers(send_n[p], recv_n).astype(bf16).astype(f32)
    own_normal, own_scale = norm_parts(own_coarse, -1)
    pulled = norm_back(delta_norm, own_normal, own_scale, -1).astype(bf16).astype(f32)
    delta_coarse = (delta_own.astype(f32) + pulled).astype(bf16)
    stripe = wm.shape[-1]
    for r in range(n_mp):
        send_c[r] = delta_coarse[:, r * stripe : (r + 1) * stripe]
    moves_c = to_peers(lambda q: send_c.at[q], columns_delta)
    columns_delta[p] = send_c[p]

    arrive(moves_e)
    recv_e[p] = send_e[p]
    output_ref[...] = (hidden + recv_e[...].astype(f32)).astype(bf16)

    arrive(moves_c)
    delta_columns = columns_delta[...].reshape(n_mp * coarse_q, stripe)
    for s in range(4):
        piece = dot(delta_columns, merge_full[s * width : (s + 1) * width], 1, 1).astype(bf16)
        send_m[:, s] = piece.reshape(n_mp, coarse_q, width)
    moves = to_peers(lambda q: send_m.at[q], recv_m)
    arrive(moves)
    delta_merged = sum_peers(send_m[p], recv_m).astype(bf16).astype(f32)
    pulled = norm_back(delta_merged, merge_normal, merge_scale, (0, 2)).astype(bf16).astype(f32)
    delta_hidden = (g_ref[...].astype(f32) + pulled).astype(bf16)
    hidden_all[p] = delta_hidden
    moves = to_peers(lambda q: hidden_all.at[p], hidden_all)
    arrive(moves)

    delta_back = dot(
        hidden_all[...].reshape(n_mp * rows_q, width), out_weight_ref[...], 1, 1
    ).astype(bf16).astype(f32)
    de[pl.ds(0, nbj), :, pl.ds(0, nbi)] = delta_back.reshape(nbj, 4, nbi, cells, local).astype(bf16)
    halo = [
        send(de.at[pl.ds(1, nbj - 1), :, 0], de.at[pl.ds(1, nbj - 1), :, nbi], plus(-1, 0, 0)),
        send(de.at[0, :, pl.ds(1, nbi - 1)], de.at[nbj, :, pl.ds(1, nbi - 1)], plus(0, -1, 0)),
        send(de.at[0, :, 0], de.at[nbj, :, nbi], plus(-1, -1, 0)),
    ]
    arrive(halo)
    delta_mixed = window_blocks(de).astype(bf16)
    for w in range(nwi * nwj):
        grads = [[], [], []]
        for h in range(heads):
            query, key, value = slices(w, h)
            scale = scale_ref[p * heads + h]
            prob = probs_ref[w * heads + h]
            delta = delta_mixed[w * window : (w + 1) * window, h * head : (h + 1) * head]
            delta_prob = dot(delta, value.astype(bf16), 1, 1).astype(bf16).astype(f32)
            delta_value = dot(prob.astype(bf16), delta, 0, 0)
            inside = jnp.sum(delta_prob * prob, -1, keepdims=True)
            delta_score = (scale * (prob * (delta_prob - inside))).astype(bf16)
            delta_query = dot(delta_score, unit(key).astype(bf16)).astype(bf16).astype(f32)
            delta_key = dot(delta_score, unit(query).astype(bf16), 0, 0).astype(bf16).astype(f32)
            grads[0].append(unit_back(delta_query, query))
            grads[1].append(unit_back(delta_key, key))
            grads[2].append(delta_value)
        attn_back[pl.ds(w * window, window), :] = jnp.concatenate(
            grads[0] + grads[1] + grads[2], 1
        ).astype(bf16)
    delta_normed = dot(attn_back[...], joined_ref[...], 1, 1)
    for index in range(nbi * nbj):
        bj, bi = block_at(index)
        block = delta_normed[index * block_rows : (index + 1) * block_rows]
        send_l[bj % n_mp, :, bi - 1] = block.reshape(4, cells, width).astype(bf16)
    moves = to_peers(lambda q: send_l.at[q], recv_l)
    column = jnp.where(p == 0, n_mp, p)
    own_source = xe[column, :, pl.ds(1, nbi)].astype(f32)
    source_normal, source_scale = norm_parts(own_source, -1)
    arrive(moves)
    delta_source = sum_peers(send_l[p], recv_l).astype(bf16).astype(f32)
    delta_source = norm_back(delta_source, source_normal, source_scale, -1)
    le[:, pl.ds(1, nbi)] = delta_source.astype(bf16)

    final = count[0]
    count[0] += 2

    def last_copy(i, src, dst, device):
        return pltpu.make_async_remote_copy(
            src_ref=src,
            dst_ref=dst,
            send_sem=send_sem.at[final + i],
            recv_sem=recv_sem.at[final + i],
            device_id=device,
            device_id_type=pl.DeviceIdType.MESH,
        )

    first_column = (p == 0).astype(jnp.int32)
    corner = last_copy(0, le.at[:, nbi], le.at[:, 0], plus(1, first_column, 0))
    corner.start()
    rest = last_copy(1, le.at[:, pl.ds(1, nbi - 1)], recv_l.at[p, :, pl.ds(1, nbi - 1)], plus(0, 1, 0))

    @pl.when(p == 0)
    def _():
        rest.start()
        rest.wait()

    @pl.when(p != 0)
    def _():
        recv_l[p, :, pl.ds(1, nbi - 1)] = le[:, pl.ds(1, nbi - 1)]

    corner.wait()
    recv_l[p, :, 0] = le[:, 0]
    own_delta = recv_l[p].astype(f32).reshape(4, coarse_q, width)
    grad_ref[...] = (delta_hidden.astype(f32) + own_delta).astype(bf16)
    for copy in sent:
        copy.wait_send()


def per_device(
    sharp_resolution_vectors,
    queries_keys_weights,
    values_weights,
    attn_result_weights,
    score_factors_by_lane,
    tile_merging_weights,
    shrunk_dense_first,
    shrunk_dense_second,
    tile_unfolding_weights,
    result_gradient,
):
    levels, row_count, column_count, width = sharp_resolution_vectors.shape
    n_lat, n_lon, n_mp = (lax.axis_size(name) for name in ("lat", "lon", "mp"))
    nbi, nbj = row_count // HALF, column_count // HALF
    cells = levels * (HALF // 2) ** 2
    assert nbj == n_mp and tile_unfolding_weights.shape[1] == width

    def to_blocks(value):
        columns = value.shape[2] // HALF
        value = value.reshape(levels, nbi, HALF // 2, 2, columns, HALF // 2, 2, width)
        value = value.transpose(4, 3, 6, 1, 0, 2, 5, 7)
        return value.reshape(columns, 4, nbi, cells, width)

    def from_blocks(value):
        value = value.reshape(2, 2, nbi, levels, HALF // 2, HALF // 2, width)
        value = value.transpose(3, 2, 4, 0, 5, 1, 6)
        return value.reshape(levels, row_count, HALF, width)

    blocks = to_blocks(sharp_resolution_vectors)
    local = values_weights.shape[1]
    joined = jnp.concatenate([queries_keys_weights.reshape(width, 2 * local), values_weights], 1)
    coarse_q = nbi * cells
    rows_q = 4 * coarse_q
    gradient = to_blocks(result_gradient).reshape(4, coarse_q, width)
    weights = (tile_merging_weights, shrunk_dense_first, shrunk_dense_second, tile_unfolding_weights)
    coarse_width = n_lon * tile_unfolding_weights.shape[0]
    stripe = tile_merging_weights.shape[1]
    heads = score_factors_by_lane.shape[0] // n_mp
    window = 16 * cells
    windows = (nbi // 2) * (nbj // 2)
    vm = pltpu.VMEM
    fine = (n_mp, rows_q, width)
    coarse = (n_mp, coarse_q, coarse_width)
    quarter = (n_mp, coarse_q, width)
    grouped = (n_mp, 4, coarse_q, width)
    pieces = (n_mp, 4, nbi, cells, width)
    scratch = [
        vm((nbj + 1, 4, nbi + 1, cells, width), bf16),
        vm((nbj + 1, 4, nbi + 1, cells, local), bf16),
        vm((nbj + 1, 4, nbi + 1, cells, local), bf16),
        vm((4, nbi + 1, cells, width), bf16),
        *[vm((n_lon,) + w.shape, bf16) for w in weights],
        vm((windows * window, 3 * local), bf16),
        vm((windows * heads, window, window), f32),
        vm((windows * window, 3 * local), bf16),
        vm(fine, bf16),
        vm(fine, bf16),
        vm(grouped, bf16),
        vm((n_mp, n_mp * coarse_q, stripe), bf16),
        vm(coarse, bf16),
        vm(coarse, bf16),
        vm(coarse, bf16),
        vm(quarter, bf16),
        vm(quarter, bf16),
        vm(quarter, bf16),
        vm(coarse, bf16),
        vm(coarse, bf16),
        vm(coarse, bf16),
        vm(coarse, bf16),
        vm(coarse, bf16),
        vm((n_mp, coarse_q, stripe), bf16),
        vm((n_mp, coarse_q, stripe), bf16),
        vm(grouped, bf16),
        vm(grouped, bf16),
        vm(grouped, bf16),
        vm(pieces, bf16),
        vm(pieces, bf16),
    ]
    copies = 11 + 14 * (n_mp - 1) + 8 * (n_lon - 1)
    scratch += [
        pltpu.SemaphoreType.DMA((copies,)),
        pltpu.SemaphoreType.DMA((copies,)),
        pltpu.SemaphoreType.DMA((4,)),
    ]
    inside = pl.BlockSpec(memory_space=pltpu.VMEM)
    outside = pl.BlockSpec(memory_space=pl.ANY)
    shape = jax.ShapeDtypeStruct((4, coarse_q, width), bf16)
    output, grad = pl.pallas_call(
        functools.partial(kernel, (n_lat, n_lon, n_mp, nbi, nbj, cells)),
        out_shape=(shape, shape),
        in_specs=[inside] * 3
        + [pl.BlockSpec(memory_space=pltpu.SMEM)]
        + [outside] * 4
        + [inside],
        out_specs=(inside, inside),
        scratch_shapes=scratch,
        compiler_params=pltpu.CompilerParams(
            collective_id=0, has_side_effects=True, vmem_limit_bytes=56 * 2**20
        ),
        name="unet_step",
    )(blocks, joined, attn_result_weights, score_factors_by_lane, *weights, gradient)
    return (from_blocks(output), from_blocks(grad))


def solution(mesh):
    in_specs = (
        P(None, "lat", "lon", None),
        P(None, None, "mp"),
        P(None, "mp"),
        P("mp", None),
        P(),
        P("lon", "mp"),
        P("lon", "mp"),
        P("mp", "lon"),
        P("lon", "mp"),
        P(None, "lat", ("lon", "mp"), None),
    )
    out_specs = (P(None, "lat", ("lon", "mp"), None), P(None, "lat", ("lon", "mp"), None))
    return jax.shard_map(
        per_device, mesh=mesh, in_specs=in_specs, out_specs=out_specs, check_vma=False
    )
```

time: 327 us -> 182 us (0.56)
  the two profiles are of different devices: /device:TPU:0 before, /device:TPU:11 now
where the time goes in v2:
time: 182 us; the launch traced here: 181 us
  Pallas kernels  172 us (95%)
  local copies, waits for them, and re-layouts  7.59 us (4%)
    pallas_call x1, Pallas kernels, per_device(): pl.pallas_call(functools.partial(kernel, (n_lat, n_lon, n_mp, nbi, nbj, c...  172 us

profile of v2, /device:TPU:11, one launch (start us, length us, event | category | flops | bytes accessed | tf_op | source)
XLA Modules:
  0.0 181.3 jit_solution(9937179391160276594)
XLA Ops:
  0.6 1.2 reshape.28
  1.9 0.5 copy.20
  2.4 0.0 copy-start
  2.4 1.0 reshape.29.x_ref
  3.4 0.0 copy-done
  3.4 0.0 copy-start.3
  3.5 0.9 copy-done.3
  4.3 0.0 copy-start.1
  4.3 0.8 pad_maximum_fusion.joined_ref
  5.1 0.1 copy-done.1
  5.2 0.1 reshape.31
  5.3 0.1 copy.22
  5.4 0.7 reshape_reshape.3.g_ref
  6.1 172.3 %unet_step.1 = (bf16[4,32,512]{2,1,0:T(8,128)(2,1)}, bf16[4,32,512]{2,1,0:T(8,128)(2,1)}) custom-call(bf16[4,4,4,8,512]{4,3,2,1,0:T(8,128)(2,1)} %reshape.29.x_ref, bf16[512,384]{1,0:T(8,128)(2,1)} %pad_maximum_fusion.joined_ref, bf16[128,512]{1,0:T(8,128)(2,1)} %out_weight_ref.1, f32[8]{0:T(128)} %scale_ref.1, bf16[512,256]{1,0:T(8,128)(2,1)} %merge_ref.1, ...), custom_call_target="tpu_custom_call" | custom-call | tf_op jit(solution)/shard_map/unet_step/pallas_call | solution.py:557
  178.4 1.0 reshape.32
  179.4 0.1 copy.14
  179.5 0.0 copy-start.2
  179.5 0.7 reshape.33
  180.2 0.2 copy-done.2
  180.4 0.1 reshape.34
  180.5 0.1 copy.15
  180.6 0.7 reshape.35
  (1 shorter events, 0.0 us)
Async XLA Ops:
  2.4 1.0 copy-start
  3.4 0.9 copy-start.3
  4.3 0.9 copy-start.1
  179.5 0.9 copy-start.2

commit v3 on v2

--- a/solution.py
+++ b/solution.py
@@ -183,34 +183,87 @@
     ]
     gradient_moves = to_peers(lambda q: g_ref.at[q], delta_e)
 
-    weights = ((merge_ref, wm), (first_ref, wf), (second_ref, ws), (unfold_ref, wu))
+    owned = ((merge_ref, wm), (first_ref, wf), (second_ref, ws), (unfold_ref, wu))
     own_copies = []
-    weight_moves = []
-    for i, (src, dst) in enumerate(weights):
-        part = src.shape[0] // split
-        mine = pl.ds(pl.multiple_of(la * part, part) if split > 1 else 0, part)
+    for i, (src, dst) in enumerate(owned):
         copy = pltpu.make_async_copy(src, dst.at[lo], local_sem.at[i])
         copy.start()
         own_copies.append(copy)
-        moves = []
+    jobs = []
+    for src, dst, pieces in (
+        (merge_ref, wm, 1),
+        (first_ref, wf, 2),
+        (unfold_ref, wu, 1),
+        (second_ref, ws, 2),
+    ):
+        rows = src.shape[0] // pieces
+        for k in range(pieces):
+            jobs.append((src, dst, k * rows, rows // split))
+    relay = n_lon == 4
+    started = {}
+    across = {}
+
+    def guarded(condition, action):
+        if condition is None:
+            action()
+        else:
+            pl.when(condition)(action)
+
+    def remote(src, dst, device, i, j):
+        return pltpu.make_async_remote_copy(
+            src_ref=src,
+            dst_ref=dst,
+            send_sem=send_sem.at[i],
+            recv_sem=recv_sem.at[j],
+            device_id=device,
+            device_id_type=pl.DeviceIdType.MESH,
+        )
+
+    guarded_sends = []
+
+    def begin(i):
+        src, dst, base, part = jobs[i]
+        mine = pl.ds(pl.multiple_of(base + la * part, part) if split > 1 else base, part)
+        first_index = count[0]
+        count[0] += n_lon
+        moves = {}
         for by in range(1, n_lon):
-            moves.append(send(src.at[mine], dst.at[lo, mine], plus(0, by, 0)))
-        weight_moves.append((moves, mine))
-    across = [None] * len(weights)
+            index = first_index + by
+            copy = remote(src.at[mine], dst.at[lo, mine], plus(0, by, 0), index, index)
+            condition = None
+            if relay and by == 1:
+                condition = lo != n_lon - 1
+            if relay and by == n_lon - 1:
+                condition = lo != 0
+            guarded(condition, copy.start)
+            guarded_sends.append((condition, copy))
+            moves[by] = copy
+        started[i] = (moves, mine, first_index)
 
     def pass_on(i):
-        dst = weights[i][1]
-        moves, mine = weight_moves[i]
+        dst = jobs[i][1]
+        moves, mine, first_index = started[i]
         across[i] = []
-        for by in range(1, n_lon):
-            moves[by - 1].wait_recv()
+        for by in [2, 1, 3] if relay else range(1, n_lon):
+            owner = lax.rem(lo - by + n_lon, n_lon)
+            moves[by].wait_recv()
+            held = dst.at[owner, mine]
+            if relay and by == 2:
+                up = remote(held, held, plus(0, 1, 0), first_index, first_index + 3)
+                down = remote(held, held, plus(0, -1, 0), first_index, first_index + 1)
+                for condition, copy in ((lo == 2, up), (lo == 1, down)):
+                    guarded(condition, copy.start)
+                    guarded_sends.append((condition, copy))
             if split > 1:
-                owner = lax.rem(lo - by + n_lon, n_lon)
-                across[i].append(send(dst.at[owner, mine], dst.at[owner, mine], plus(1, 0, 0)))
-
-    def ready(i):
-        arrive(across[i])
-        own_copies[i].wait()
+                across[i].append(send(held, held, plus(1, 0, 0)))
+
+    def ready(which, numbers):
+        for i in numbers:
+            arrive(across[i])
+        own_copies[which].wait()
+
+    for i in (0, 1, 2):
+        begin(i)
 
     xe[pl.ds(0, nbj), :, pl.ds(0, nbi)] = x_ref[...]
     arrive(halo)
@@ -278,12 +331,13 @@
         send(me.at[nbj, :, nbi], me.at[0, :, 0], plus(1, 1, 0)),
     ]
     pass_on(0)
+    for i in (3, 4, 5):
+        begin(i)
     arrive(back)
     mixed_back = me[pl.ds(0, nbj), :, pl.ds(0, nbi)].astype(f32).reshape(n_mp * rows_q, local)
     partial = dot(mixed_back.astype(bf16), out_weight_ref[...]).astype(bf16)
     send_a[...] = partial.reshape(n_mp, rows_q, width)
     moves = to_peers(lambda q: send_a.at[q], recv_a)
-    pass_on(1)
     arrive(moves)
     own_fine = x_ref[p].astype(f32).reshape(rows_q, width)
     hidden = (own_fine + sum_peers(send_a[p], recv_a)).astype(bf16)
@@ -291,7 +345,8 @@
     merge_normal, merge_scale = norm_parts(hidden, (0, 2))
     merged_all[p] = merge_normal.astype(bf16)
     moves = to_peers(lambda q: merged_all.at[p], merged_all)
-    ready(0)
+    pass_on(1)
+    ready(0, (0,))
     merge_full = wm[...].reshape(4 * width, wm.shape[-1])
     arrive(moves)
     columns = jnp.zeros((n_mp * coarse_q, wm.shape[-1]), f32)
@@ -301,7 +356,6 @@
     columns_all[p] = columns.astype(bf16)
     moves = to_peers(lambda q: columns_all.at[p], columns_all)
     pass_on(2)
-    pass_on(3)
 
     for q in range(n_mp):
         @pl.when(p == q)
@@ -309,7 +363,8 @@
             delta_e[q] = g_ref[q]
 
     arrive(gradient_moves)
-    ready(3)
+    pass_on(3)
+    ready(3, (3,))
     tokens_delta = delta_e[...].reshape(n_mp * coarse_q, width)
     unfold_full = wu[...].reshape(n_lon * wu.shape[1], width)
     coarse_width = unfold_full.shape[0]
@@ -320,19 +375,20 @@
     arrive(moves)
     coarse = jnp.concatenate([columns_all[r] for r in range(n_mp)], 1).astype(f32)
     coarse_norm = norm_parts(coarse, -1)[0].astype(bf16)
-    ready(1)
+    ready(1, (1, 2))
     first_full = wf[...].reshape(coarse_width, wf.shape[-1])
     inner = dot(coarse_norm, first_full).astype(bf16).astype(f32)
     activated = gelu(inner).astype(bf16)
-    ready(2)
-    outer = jnp.concatenate([dot(activated, ws[k]) for k in range(n_lon)], 1).astype(bf16)
-    send_o[...] = outer.reshape(n_mp, coarse_q, coarse_width)
-    moves_o = to_peers(lambda q: send_o.at[q], recv_o)
-
+    pass_on(4)
     arrive(moves_d)
     delta_own = sum_peers(send_d[p], recv_d).astype(bf16)
     delta_all[p] = delta_own
     moves_d = to_peers(lambda q: delta_all.at[p], delta_all)
+    pass_on(5)
+    ready(2, (4, 5))
+    outer = jnp.concatenate([dot(activated, ws[k]) for k in range(n_lon)], 1).astype(bf16)
+    send_o[...] = outer.reshape(n_mp, coarse_q, coarse_width)
+    moves_o = to_peers(lambda q: send_o.at[q], recv_o)
 
     arrive(moves_o)
     own_coarse = jnp.concatenate(
@@ -464,6 +520,8 @@
     grad_ref[...] = (delta_hidden.astype(f32) + own_delta).astype(bf16)
     for copy in sent:
         copy.wait_send()
+    for condition, copy in guarded_sends:
+        guarded(condition, copy.wait_send)
 
 
 def per_device(
@@ -545,7 +603,7 @@
         vm(pieces, bf16),
         vm(pieces, bf16),
     ]
-    copies = 11 + 14 * (n_mp - 1) + 8 * (n_lon - 1)
+    copies = 11 + 14 * (n_mp - 1) + 12 * n_lon
     scratch += [
         pltpu.SemaphoreType.DMA((copies,)),
         pltpu.SemaphoreType.DMA((copies,)),

time: 182 us -> 156 us (0.86)
  the two profiles are of different devices: /device:TPU:11 before, /device:TPU:0 now
where the time goes in v3:
time: 156 us
  Pallas kernels  147 us (94%)
  local copies, waits for them, and re-layouts  7.59 us (5%)
    pallas_call x1, Pallas kernels, per_device(): pl.pallas_call(functools.partial(kernel, (n_lat, n_lon, n_mp, nbi, nbj, c...  147 us

profile of v3, /device:TPU:0, one launch (start us, length us, event | category | flops | bytes accessed | tf_op | source)
XLA Modules:
  0.0 156.0 jit_solution(10730829161326597655)
XLA Ops:
  0.6 1.2 reshape.28
  1.9 0.5 copy.20
  2.4 0.0 copy-start
  2.4 1.0 reshape.29.x_ref
  3.4 0.0 copy-done
  3.4 0.0 copy-start.3
  3.5 0.9 copy-done.3
  4.3 0.0 copy-start.1
  4.3 0.8 pad_maximum_fusion.joined_ref
  5.1 0.1 copy-done.1
  5.2 0.1 reshape.31
  5.3 0.1 copy.22
  5.4 0.7 reshape_reshape.3.g_ref
  6.1 146.9 %unet_step.1 = (bf16[4,32,512]{2,1,0:T(8,128)(2,1)}, bf16[4,32,512]{2,1,0:T(8,128)(2,1)}) custom-call(bf16[4,4,4,8,512]{4,3,2,1,0:T(8,128)(2,1)} %reshape.29.x_ref, bf16[512,384]{1,0:T(8,128)(2,1)} %pad_maximum_fusion.joined_ref, bf16[128,512]{1,0:T(8,128)(2,1)} %out_weight_ref.1, f32[8]{0:T(128)} %scale_ref.1, bf16[512,256]{1,0:T(8,128)(2,1)} %merge_ref.1, ...), custom_call_target="tpu_custom_call" | custom-call | tf_op jit(solution)/shard_map/unet_step/pallas_call | solution.py:615
  153.1 1.0 reshape.32
  154.0 0.1 copy.14
  154.2 0.0 copy-start.2
  154.2 0.7 reshape.33
  154.9 0.2 copy-done.2
  155.1 0.1 reshape.34
  155.1 0.1 copy.15
  155.3 0.7 reshape.35
  (1 shorter events, 0.0 us)
Async XLA Ops:
  2.4 1.0 copy-start
  3.4 0.9 copy-start.3
  4.3 0.9 copy-start.1
  154.2 0.9 copy-start.2

commit v4 on v3

--- a/solution.py
+++ b/solution.py
@@ -305,6 +305,7 @@
 
         return part(0), part(1), part(2)
 
+    pass_on(0)
     mixed_windows = []
     for w in range(nwi * nwj):
         per_head = []
@@ -330,7 +331,7 @@
         send(me.at[nbj, :, pl.ds(1, nbi - 1)], me.at[0, :, pl.ds(1, nbi - 1)], plus(0, 1, 0)),
         send(me.at[nbj, :, nbi], me.at[0, :, 0], plus(1, 1, 0)),
     ]
-    pass_on(0)
+    pass_on(1)
     for i in (3, 4, 5):
         begin(i)
     arrive(back)
@@ -345,7 +346,7 @@
     merge_normal, merge_scale = norm_parts(hidden, (0, 2))
     merged_all[p] = merge_normal.astype(bf16)
     moves = to_peers(lambda q: merged_all.at[p], merged_all)
-    pass_on(1)
+    pass_on(2)
     ready(0, (0,))
     merge_full = wm[...].reshape(4 * width, wm.shape[-1])
     arrive(moves)
@@ -355,7 +356,7 @@
         columns = columns + dot(tokens, merge_full[s * width : (s + 1) * width])
     columns_all[p] = columns.astype(bf16)
     moves = to_peers(lambda q: columns_all.at[p], columns_all)
-    pass_on(2)
+    pass_on(3)
 
     for q in range(n_mp):
         @pl.when(p == q)
@@ -363,7 +364,6 @@
             delta_e[q] = g_ref[q]
 
     arrive(gradient_moves)
-    pass_on(3)
     ready(3, (3,))
     tokens_delta = delta_e[...].reshape(n_mp * coarse_q, width)
     unfold_full = wu[...].reshape(n_lon * wu.shape[1], width)

time: 156 us -> 146 us (0.936)
  Pallas kernels: 147 us -> 137 us
    pallas_call x1, Pallas kernels: 147 us -> 137 us  [per_device(): pl.pallas_call(functools.partial(kernel, (n_lat, n_lon, n_mp, nbi, nbj, c...]
where the time goes in v4:
time: 146 us
  Pallas kernels  137 us (94%)
  local copies, waits for them, and re-layouts  7.59 us (5%)
    pallas_call x1, Pallas kernels, per_device(): pl.pallas_call(functools.partial(kernel, (n_lat, n_lon, n_mp, nbi, nbj, c...  137 us

profile of v4, /device:TPU:0, one launch (start us, length us, event | category | flops | bytes accessed | tf_op | source)
XLA Modules:
  0.0 146.0 jit_solution(18236128745344186876)
XLA Ops:
  0.6 1.2 reshape.28
  1.9 0.5 copy.20
  2.4 0.0 copy-start
  2.4 1.0 reshape.29.x_ref
  3.4 0.0 copy-done
  3.4 0.0 copy-start.3
  3.5 0.9 copy-done.3
  4.3 0.0 copy-start.1
  4.3 0.8 pad_maximum_fusion.joined_ref
  5.1 0.1 copy-done.1
  5.2 0.1 reshape.31
  5.3 0.1 copy.22
  5.4 0.7 reshape_reshape.3.g_ref
  6.1 136.9 %unet_step.1 = (bf16[4,32,512]{2,1,0:T(8,128)(2,1)}, bf16[4,32,512]{2,1,0:T(8,128)(2,1)}) custom-call(bf16[4,4,4,8,512]{4,3,2,1,0:T(8,128)(2,1)} %reshape.29.x_ref, bf16[512,384]{1,0:T(8,128)(2,1)} %pad_maximum_fusion.joined_ref, bf16[128,512]{1,0:T(8,128)(2,1)} %out_weight_ref.1, f32[8]{0:T(128)} %scale_ref.1, bf16[512,256]{1,0:T(8,128)(2,1)} %merge_ref.1, ...), custom_call_target="tpu_custom_call" | custom-call | tf_op jit(solution)/shard_map/unet_step/pallas_call | solution.py:615
  143.1 1.0 reshape.32
  144.0 0.1 copy.14
  144.2 0.0 copy-start.2
  144.2 0.7 reshape.33
  144.9 0.2 copy-done.2
  145.1 0.1 reshape.34
  145.2 0.1 copy.15
  145.3 0.7 reshape.35
  (1 shorter events, 0.0 us)
Async XLA Ops:
  2.4 1.0 copy-start
  3.4 0.9 copy-start.3
  4.3 0.9 copy-start.1
  144.2 0.9 copy-start.2
